TPU v7x, 512 devices: a whole 4x4x16 slice. The times are simulated.
512 devices in a mesh: ctx: 64 (over z, y), head: 8 (over x, core).
Axes of the slice: x: 4, y: 4, z: 16, core: 2. Of those that a mesh axis runs over, the one named last changes fastest.
Arguments:
- queries: bfloat16 [32768, 1024], P('ctx', 'head'), may hold values from -6 to 6
- keys: bfloat16 [32768, 1024], P('ctx', 'head'), may hold values from -6 to 6
- values: bfloat16 [32768, 1024], P('ctx', 'head'), may hold values from -6 to 6
- out_grad: bfloat16 [32768, 1024], P('ctx', 'head'), may hold values from -12 to 12
- cluster_ids: int32 [512], P('ctx'), may hold values from 0 to 255, as said below
Outputs:
- queries_grad: bfloat16 [32768, 1024], P('ctx', 'head')
- keys_grad: bfloat16 [32768, 1024], P('ctx', 'head')
- values_grad: bfloat16 [32768, 1024], P('ctx', 'head')
- centroids: float32 [256, 128], P('ctx')
Inputs may be any that keep to these rules, and one draw needn't show every extreme that they name: `cluster_ids`: cluster c is owned by index c // 4 of ctx. The 8 blocks of one index of ctx go 1 at a time: exactly 1 of them to each of 8 owners and none to the others; every owner receives exactly 8 blocks.
All inputs are finite; a program needn't handle non-finite values.
Results may differ from a plain program's by a relative error of at most 0.012.
The roundings to bfloat16 on the way count: a program that leaves them out, or rounds other values in their place, can miss the bound.
Values may be sent and summed in bfloat16 or wider, within the bound.
A program may use at most 64 MiB of HBM per device.

v0:
```python
import math

import jax
import jax.numpy as jnp
from jax import lax
from jax.sharding import PartitionSpec as P

HDIM = 128
CLUS_DEV = 4


def masked_scores(q_tile, k_keys, row_cluster, first_row, score_scale):
    count = q_tile.shape[0]
    extent = k_keys.shape[0]
    product = (
        jnp.einsum("qd,kd->qk", q_tile, k_keys, preferred_element_type=jnp.float32) * score_scale
    )
    query_pos = first_row + jnp.arange(count)
    key_pos = jnp.arange(extent)
    allowed = (row_cluster[:, None] == row_cluster[None, :]) & (
        key_pos[None, :] <= query_pos[:, None]
    )
    return jnp.where(allowed, product, -jnp.inf)


def shards(queries, keys, values, out_grad, cluster_ids):
    blocks = cluster_ids.shape[0]
    rows_dev, width = queries.shape
    block_rows = rows_dev // blocks
    owners = lax.axis_size("ctx")
    per_owner = max(1, 2 * blocks // owners)
    slot_count = owners * per_owner
    owner_dev = cluster_ids // CLUS_DEV
    within = jnp.arange(blocks)
    earlier = jnp.sum(
        ((owner_dev[None, :] == owner_dev[:, None]) & (within[None, :] < within[:, None])).astype(
            jnp.int32
        ),
        axis=1,
    )
    target = owner_dev * per_owner + earlier

    def pack(source):
        return (
            jnp.zeros((slot_count, block_rows, width), source.dtype)
            .at[target]
            .set(source.reshape(blocks, block_rows, width))
        )

    labels = jnp.full((slot_count,), -1, jnp.int32).at[target].set(cluster_ids)
    q_in, k_in, v_in, g_in, label_in = (
        lax.all_to_all(pack(queries), "ctx", split_axis=0, concat_axis=0, tiled=True),
        lax.all_to_all(pack(keys), "ctx", split_axis=0, concat_axis=0, tiled=True),
        lax.all_to_all(pack(values), "ctx", split_axis=0, concat_axis=0, tiled=True),
        lax.all_to_all(pack(out_grad), "ctx", split_axis=0, concat_axis=0, tiled=True),
        lax.all_to_all(labels, "ctx", split_axis=0, concat_axis=0, tiled=True),
    )
    picked = jnp.argsort(jnp.where(label_in >= 0, 0, 1), stable=True)[:blocks]
    row_total = blocks * block_rows

    def compact(arrived):
        return arrived[picked].reshape(row_total, width)

    q_own = compact(q_in)
    k_own = compact(k_in)
    v_own = compact(v_in)
    row_cluster = jnp.repeat(label_in[picked], block_rows)
    score_scale = 1.0 / math.sqrt(HDIM)
    tile_rows = math.gcd(row_total, 512)
    tile_starts = list(range(0, row_total, tile_rows))
    heads_local = width // HDIM
    g_own = compact(g_in)
    grads_q, grads_k, grads_v = ([], [], [])
    keys_acc = jnp.zeros((row_total, HDIM), jnp.float32)
    values_acc = jnp.zeros((row_total, HDIM), jnp.float32)
    query_tiles = []
    for first_row in tile_starts:
        scores = masked_scores(q_own, k_own, row_cluster, first_row, score_scale)
        row_peak = jnp.max(scores, axis=1, keepdims=True)
        exponent = jnp.exp(scores - row_peak)
        probs = exponent / jnp.sum(exponent, axis=1, keepdims=True)
        probs_low = probs.astype(jnp.bfloat16)
        attn_out = jnp.dot(probs_low, v_own, preferred_element_type=jnp.float32)
        delta_row = jnp.sum(g_own.astype(jnp.float32) * attn_out, axis=1, keepdims=True)
        values_acc = values_acc.at[:row_total].add(
            jnp.einsum("qk,qd->kd", probs_low, g_own, preferred_element_type=jnp.float32)
        )
        dprob = jnp.einsum("qd,kd->qk", g_own, v_own, preferred_element_type=jnp.float32)
        dscore = (probs * (dprob - delta_row)).astype(jnp.bfloat16)
        query_tiles.append(jnp.dot(dscore, k_own, preferred_element_type=jnp.float32) * score_scale)
        keys_acc = keys_acc.at[:row_total].add(
            jnp.einsum("qk,qd->kd", dscore, q_own, preferred_element_type=jnp.float32)
        )
    grads_q.append(query_tiles[0].astype(jnp.bfloat16))
    grads_k.append((keys_acc * score_scale).astype(jnp.bfloat16))
    grads_v.append(values_acc.astype(jnp.bfloat16))
    grad_q_own = grads_q[0]
    grad_k_own = grads_k[0]
    grad_v_own = grads_v[0]

    def spread(result):
        return (
            jnp.zeros((slot_count, block_rows, width), jnp.bfloat16)
            .at[picked]
            .set(result.reshape(blocks, block_rows, width))
        )

    back_q, back_k, back_v = (
        lax.all_to_all(spread(grad_q_own), "ctx", split_axis=0, concat_axis=0, tiled=True),
        lax.all_to_all(spread(grad_k_own), "ctx", split_axis=0, concat_axis=0, tiled=True),
        lax.all_to_all(spread(grad_v_own), "ctx", split_axis=0, concat_axis=0, tiled=True),
    )

    def restore(arrived):
        return arrived[target].reshape(rows_dev, width)

    key_heads = k_own.astype(jnp.float32).reshape(row_total, heads_local, HDIM).sum(axis=1)
    member = ((row_cluster % CLUS_DEV)[None, :] == jnp.arange(CLUS_DEV)[:, None]).astype(
        jnp.float32
    )
    partial_sums = jnp.dot(member, key_heads, precision=lax.Precision.HIGHEST)
    whole_sums = lax.psum(partial_sums, "head")
    centroids = whole_sums / jnp.sqrt(
        jnp.mean(whole_sums * whole_sums, axis=1, keepdims=True) + 1e-06
    )
    return (restore(back_q), restore(back_k), restore(back_v), centroids)


def solution(mesh):
    placed = (P("ctx", "head"), P("ctx", "head"), P("ctx", "head"), P("ctx", "head"), P("ctx"))
    return jax.shard_map(
        shards,
        mesh=mesh,
        in_specs=placed,
        out_specs=(P("ctx", "head"), P("ctx", "head"), P("ctx", "head"), P("ctx", None)),
        check_vma=False,
    )
```

profile of v0, /device:TPU:6, one launch (start us, length us, event | category | flops | bytes accessed | tf_op | source)
XLA Modules:
  0.0 458.8 jit_solution(8997567611046990863)
XLA Ops:
  3.3 18.7 %all-to-all-start = ((s32[64,1,1]{2,1,0:T(1,128)}), s32[64,1,1]{2,1,0:T(1,128)S(1)}, u32[]{:S(2)}, u32[]{:S(2)}) async-start(s32[64,1,1]{2,1,0:T(1,128)} %copy.23), calls=%async_computation | async-start | bytes 65536 | tf_op jit(solution)/shard_map/all_to_all | solution.py:56
  22.0 1.3 broadcast.128.clone.1
  23.3 2.1 scatter_fusion.1
  25.4 11.2 %all-to-all-done = s32[64,1,1]{2,1,0:T(1,128)S(1)} async-done(((s32[64,1,1]{2,1,0:T(1,128)}), s32[64,1,1]{2,1,0:T(1,128)S(1)}, u32[]{:S(2)}, u32[]{:S(2)}) %all-to-all-start) | async-done | bytes 288 | tf_op jit(solution)/shard_map/all_to_all | solution.py:56
  36.5 4.7 %all-to-all-start.2 = ((bf16[64,64,128]{2,1,0:T(8,128)(2,1)}), bf16[64,64,128]{2,1,0:T(8,128)(2,1)S(1)}, u32[]{:S(2)}, u32[]{:S(2)}) async-start(bf16[64,64,128]{2,1,0:T(8,128)(2,1)} %scatter_fusion.1), calls=%async_computation.2 | async-start | bytes 2097152 | tf_op jit(solution)/shard_map/all_to_all | solution.py:53
  41.2 1.2 broadcast.128.clone.2
  42.5 2.1 scatter_fusion
  44.5 50.8 %all-to-all-done.2 = bf16[64,64,128]{2,1,0:T(8,128)(2,1)S(1)} async-done(((bf16[64,64,128]{2,1,0:T(8,128)(2,1)}), bf16[64,64,128]{2,1,0:T(8,128)(2,1)S(1)}, u32[]{:S(2)}, u32[]{:S(2)}) %all-to-all-start.2) | async-done | bytes 1048608 | tf_op jit(solution)/shard_map/all_to_all | solution.py:53
  95.3 5.8 %all-to-all-start.1 = ((bf16[64,64,128]{2,1,0:T(8,128)(2,1)}), bf16[64,64,128]{2,1,0:T(8,128)(2,1)S(1)}, u32[]{:S(2)}, u32[]{:S(2)}) async-start(bf16[64,64,128]{2,1,0:T(8,128)(2,1)} %scatter_fusion), calls=%async_computation.1 | async-start | bytes 2097152 | tf_op jit(solution)/shard_map/all_to_all | solution.py:52
  101.2 1.3 broadcast.128.clone.4
  102.5 2.1 scatter_fusion.2
  104.6 51.0 %all-to-all-done.1 = bf16[64,64,128]{2,1,0:T(8,128)(2,1)S(1)} async-done(((bf16[64,64,128]{2,1,0:T(8,128)(2,1)}), bf16[64,64,128]{2,1,0:T(8,128)(2,1)S(1)}, u32[]{:S(2)}, u32[]{:S(2)}) %all-to-all-start.1) | async-done | bytes 1048608 | tf_op jit(solution)/shard_map/all_to_all | solution.py:52
  155.6 5.8 %all-to-all-start.3 = ((bf16[64,64,128]{2,1,0:T(8,128)(2,1)}), bf16[64,64,128]{2,1,0:T(8,128)(2,1)S(1)}, u32[]{:S(2)}, u32[]{:S(2)}) async-start(bf16[64,64,128]{2,1,0:T(8,128)(2,1)} %scatter_fusion.2), calls=%async_computation.3 | async-start | bytes 2097152 | tf_op jit(solution)/shard_map/all_to_all | solution.py:55
  161.4 1.2 broadcast.128.clone.3
  162.7 2.1 scatter_fusion.3
  164.8 50.2 %all-to-all-done.3 = bf16[64,64,128]{2,1,0:T(8,128)(2,1)S(1)} async-done(((bf16[64,64,128]{2,1,0:T(8,128)(2,1)}), bf16[64,64,128]{2,1,0:T(8,128)(2,1)S(1)}, u32[]{:S(2)}, u32[]{:S(2)}) %all-to-all-start.3) | async-done | bytes 1048608 | tf_op jit(solution)/shard_map/all_to_all | solution.py:55
  216.0 5.8 %all-to-all-start.4 = ((bf16[64,64,128]{2,1,0:T(8,128)(2,1)}), bf16[64,64,128]{2,1,0:T(8,128)(2,1)S(1)}, u32[]{:S(2)}, u32[]{:S(2)}) async-start(bf16[64,64,128]{2,1,0:T(8,128)(2,1)} %scatter_fusion.3), calls=%async_computation.4 | async-start | bytes 2097152 | tf_op jit(solution)/shard_map/all_to_all | solution.py:54
  223.1 2.0 sort.17
  227.2 1.8 gather_fusion.3
  231.6 43.4 %all-to-all-done.4 = bf16[64,64,128]{2,1,0:T(8,128)(2,1)S(1)} async-done(((bf16[64,64,128]{2,1,0:T(8,128)(2,1)}), bf16[64,64,128]{2,1,0:T(8,128)(2,1)S(1)}, u32[]{:S(2)}, u32[]{:S(2)}) %all-to-all-start.4) | async-done | bytes 1048608 | tf_op jit(solution)/shard_map/all_to_all | solution.py:54
  277.5 1.3 broadcast.128.clone
  278.8 2.1 scatter_fusion.4
  280.9 6.0 %all-to-all-start.5 = ((bf16[64,64,128]{2,1,0:T(8,128)(2,1)}), bf16[64,64,128]{2,1,0:T(8,128)(2,1)S(1)}, u32[]{:S(2)}, u32[]{:S(2)}) async-start(bf16[64,64,128]{2,1,0:T(8,128)(2,1)} %scatter_fusion.4), calls=%async_computation.5 | async-start | bytes 2097152 | tf_op jit(solution)/shard_map/all_to_all | solution.py:109
  288.5 2.1 scatter_fusion.5
  290.5 49.3 %all-to-all-done.5 = bf16[64,64,128]{2,1,0:T(8,128)(2,1)S(1)} async-done(((bf16[64,64,128]{2,1,0:T(8,128)(2,1)}), bf16[64,64,128]{2,1,0:T(8,128)(2,1)S(1)}, u32[]{:S(2)}, u32[]{:S(2)}) %all-to-all-start.5) | async-done | bytes 1048608 | tf_op jit(solution)/shard_map/all_to_all | solution.py:109
  339.8 5.8 %all-to-all-start.6 = ((bf16[64,64,128]{2,1,0:T(8,128)(2,1)}), bf16[64,64,128]{2,1,0:T(8,128)(2,1)S(1)}, u32[]{:S(2)}, u32[]{:S(2)}) async-start(bf16[64,64,128]{2,1,0:T(8,128)(2,1)} %scatter_fusion.5), calls=%async_computation.6 | async-start | bytes 2097152 | tf_op jit(solution)/shard_map/all_to_all | solution.py:110
  345.9 1.3 broadcast.128.clone.6
  347.2 2.1 scatter_fusion.6
  349.3 49.4 %all-to-all-done.6 = bf16[64,64,128]{2,1,0:T(8,128)(2,1)S(1)} async-done(((bf16[64,64,128]{2,1,0:T(8,128)(2,1)}), bf16[64,64,128]{2,1,0:T(8,128)(2,1)S(1)}, u32[]{:S(2)}, u32[]{:S(2)}) %all-to-all-start.6) | async-done | bytes 1048608 | tf_op jit(solution)/shard_map/all_to_all | solution.py:110
  398.7 5.8 %all-to-all-start.7 = ((bf16[64,64,128]{2,1,0:T(8,128)(2,1)}), bf16[64,64,128]{2,1,0:T(8,128)(2,1)S(1)}, u32[]{:S(2)}, u32[]{:S(2)}) async-start(bf16[64,64,128]{2,1,0:T(8,128)(2,1)} %scatter_fusion.6), calls=%async_computation.7 | async-start | bytes 2097152 | tf_op jit(solution)/shard_map/all_to_all | solution.py:111
  404.7 10.6 %psum.7 = f32[4,128]{1,0:T(4,128)S(1)} all-reduce(f32[4,128]{1,0:T(4,128)S(1)} %fusion.15), channel_id=1, replica_groups=mesh['ctx'=64,'head'=8] {'head'}, use_global_device_ids=true, to_apply=%region_13.14 | all-reduce | flops 512 | bytes 4096 | tf_op jit(solution)/shard_map/psum | solution.py:122
  418.5 39.1 %all-to-all-done.7 = bf16[64,64,128]{2,1,0:T(8,128)(2,1)S(1)} async-done(((bf16[64,64,128]{2,1,0:T(8,128)(2,1)}), bf16[64,64,128]{2,1,0:T(8,128)(2,1)S(1)}, u32[]{:S(2)}, u32[]{:S(2)}) %all-to-all-start.7) | async-done | bytes 1048608 | tf_op jit(solution)/shard_map/all_to_all | solution.py:111
  (52 shorter events, 18.5 us)
Async XLA Ops:
  1.3 0.7 copy-start.7
  3.3 33.3 %all-to-all-start = ((s32[64,1,1]{2,1,0:T(1,128)}), s32[64,1,1]{2,1,0:T(1,128)S(1)}, u32[]{:S(2)}, u32[]{:S(2)}) async-start(s32[64,1,1]{2,1,0:T(1,128)} %copy.23), calls=%async_computation | async-start | bytes 65536 | tf_op jit(solution)/shard_map/all_to_all | solution.py:56
  22.0 1.3 copy-start.2
  36.5 58.8 %all-to-all-start.2 = ((bf16[64,64,128]{2,1,0:T(8,128)(2,1)}), bf16[64,64,128]{2,1,0:T(8,128)(2,1)S(1)}, u32[]{:S(2)}, u32[]{:S(2)}) async-start(bf16[64,64,128]{2,1,0:T(8,128)(2,1)} %scatter_fusion.1), calls=%async_computation.2 | async-start | bytes 2097152 | tf_op jit(solution)/shard_map/all_to_all | solution.py:53
  41.2 1.3 copy-start.3
  95.3 60.2 %all-to-all-start.1 = ((bf16[64,64,128]{2,1,0:T(8,128)(2,1)}), bf16[64,64,128]{2,1,0:T(8,128)(2,1)S(1)}, u32[]{:S(2)}, u32[]{:S(2)}) async-start(bf16[64,64,128]{2,1,0:T(8,128)(2,1)} %scatter_fusion), calls=%async_computation.1 | async-start | bytes 2097152 | tf_op jit(solution)/shard_map/all_to_all | solution.py:52
  101.2 1.3 copy-start.4
  155.6 59.4 %all-to-all-start.3 = ((bf16[64,64,128]{2,1,0:T(8,128)(2,1)}), bf16[64,64,128]{2,1,0:T(8,128)(2,1)S(1)}, u32[]{:S(2)}, u32[]{:S(2)}) async-start(bf16[64,64,128]{2,1,0:T(8,128)(2,1)} %scatter_fusion.2), calls=%async_computation.3 | async-start | bytes 2097152 | tf_op jit(solution)/shard_map/all_to_all | solution.py:55
  161.4 1.3 copy-start.5
  215.0 1.0 copy-start
  216.0 59.0 %all-to-all-start.4 = ((bf16[64,64,128]{2,1,0:T(8,128)(2,1)}), bf16[64,64,128]{2,1,0:T(8,128)(2,1)S(1)}, u32[]{:S(2)}, u32[]{:S(2)}) async-start(bf16[64,64,128]{2,1,0:T(8,128)(2,1)} %scatter_fusion.3), calls=%async_computation.4 | async-start | bytes 2097152 | tf_op jit(solution)/shard_map/all_to_all | solution.py:54
  231.6 44.0 %copy-start.6 = (bf16[512,128]{0,1:T(8,128)(2,1)S(1)}, bf16[512,128]{0,1:T(8,128)(2,1)}, u32[]{:S(2)}) copy-start(bf16[512,128]{0,1:T(8,128)(2,1)} %copy.24) | copy-start | bytes 393220
  275.5 1.0 copy-start.1
  280.9 58.9 %all-to-all-start.5 = ((bf16[64,64,128]{2,1,0:T(8,128)(2,1)}), bf16[64,64,128]{2,1,0:T(8,128)(2,1)S(1)}, u32[]{:S(2)}, u32[]{:S(2)}) async-start(bf16[64,64,128]{2,1,0:T(8,128)(2,1)} %scatter_fusion.4), calls=%async_computation.5 | async-start | bytes 2097152 | tf_op jit(solution)/shard_map/all_to_all | solution.py:109
  339.8 58.9 %all-to-all-start.6 = ((bf16[64,64,128]{2,1,0:T(8,128)(2,1)}), bf16[64,64,128]{2,1,0:T(8,128)(2,1)S(1)}, u32[]{:S(2)}, u32[]{:S(2)}) async-start(bf16[64,64,128]{2,1,0:T(8,128)(2,1)} %scatter_fusion.5), calls=%async_computation.6 | async-start | bytes 2097152 | tf_op jit(solution)/shard_map/all_to_all | solution.py:110
  398.7 58.9 %all-to-all-start.7 = ((bf16[64,64,128]{2,1,0:T(8,128)(2,1)}), bf16[64,64,128]{2,1,0:T(8,128)(2,1)S(1)}, u32[]{:S(2)}, u32[]{:S(2)}) async-start(bf16[64,64,128]{2,1,0:T(8,128)(2,1)} %scatter_fusion.6), calls=%async_computation.7 | async-start | bytes 2097152 | tf_op jit(solution)/shard_map/all_to_all | solution.py:111
where the time goes:
time: 461 us; the launch traced here: 459 us
  waiting for transfers between devices  344 us (75%)
  starting transfers between devices  58.6 us (13%)
  local copies, waits for them, and re-layouts  36.4 us (8%)
  blocking collectives  10.6 us (2%)
  other arithmetic  5.44 us (1%)
    all_to_all x1, waiting for transfers between devices, shards(): lax.all_to_all(pack(queries), 'ctx', split_axis=0, concat_axis=0, tiled=T...  51 us
    all_to_all x1, waiting for transfers between devices, shards(): lax.all_to_all(pack(keys), 'ctx', split_axis=0, concat_axis=0, tiled=True)  50.8 us
    all_to_all x1, waiting for transfers between devices, shards(): lax.all_to_all(pack(out_grad), 'ctx', split_axis=0, concat_axis=0, tiled=...  50.2 us
    all_to_all x1, waiting for transfers between devices, shards(): lax.all_to_all(spread(grad_k_own), 'ctx', split_axis=0, concat_axis=0, ti...  49.4 us
    all_to_all x1, waiting for transfers between devices, shards(): lax.all_to_all(spread(grad_q_own), 'ctx', split_axis=0, concat_axis=0, ti...  49.3 us
    all_to_all x1, waiting for transfers between devices, shards(): lax.all_to_all(pack(values), 'ctx', split_axis=0, concat_axis=0, tiled=True)  43.4 us
    all_to_all x1, waiting for transfers between devices, shards(): lax.all_to_all(spread(grad_v_own), 'ctx', split_axis=0, concat_axis=0, ti...  39.1 us
    all_to_all x1, starting transfers between devices, shards(): lax.all_to_all(labels, 'ctx', split_axis=0, concat_axis=0, tiled=True)  18.7 us
  transfers between devices with their start and end apart: 8, of which 8 were waited for; matrix products, arithmetic and copies ran while one was open for 7% of the time, Pallas kernels for 0%

commit v1 on v0

v1 whole, which is shorter than its diff:
```python
import math

import jax
import jax.numpy as jnp
from jax import lax
from jax.sharding import PartitionSpec as P

HDIM = 128
CLUS_DEV = 4


def exchange(pieces):
    return lax.all_to_all(pieces, "ctx", split_axis=0, concat_axis=0, tiled=True)


def shards(queries, keys, values, out_grad, cluster_ids):
    blocks = cluster_ids.shape[0]
    rows_dev, width = queries.shape
    block_rows = rows_dev // blocks
    owners = lax.axis_size("ctx")
    me = lax.axis_index("ctx")
    all_ids = lax.all_gather(cluster_ids, "ctx", tiled=True)
    order = jnp.argsort(all_ids // CLUS_DEV, stable=True)
    place = jnp.argsort(order, stable=True)
    row_ids = lax.dynamic_slice_in_dim(all_ids[order], me * blocks, blocks)

    sent = jnp.stack(
        [a.reshape(blocks, block_rows, width) for a in (queries, keys, values, out_grad)], axis=2
    )
    held = exchange(sent.swapaxes(0, 1).reshape(owners, blocks, 4 * width))
    held = held.reshape(owners * blocks, 4 * width)[order]
    own = exchange(held.reshape(owners, blocks, 4 * width))
    own = own.swapaxes(0, 1).reshape(rows_dev, 4 * width)
    q_own, k_own, v_own, g_own = jnp.split(own, 4, axis=1)

    score_scale = 1.0 / math.sqrt(HDIM)
    row_cluster = jnp.repeat(row_ids, block_rows)
    position = jnp.arange(rows_dev)
    allowed = (row_cluster[:, None] == row_cluster[None, :]) & (
        position[None, :] <= position[:, None]
    )
    scores = jnp.einsum("qd,kd->qk", q_own, k_own, preferred_element_type=jnp.float32)
    scores = jnp.where(allowed, scores * score_scale, -jnp.inf)
    exponent = jnp.exp(scores - jnp.max(scores, axis=1, keepdims=True))
    probs = exponent / jnp.sum(exponent, axis=1, keepdims=True)
    probs_low = probs.astype(jnp.bfloat16)
    attn_out = jnp.dot(probs_low, v_own, preferred_element_type=jnp.float32)
    delta_row = jnp.sum(g_own.astype(jnp.float32) * attn_out, axis=1, keepdims=True)
    grad_v = jnp.einsum("qk,qd->kd", probs_low, g_own, preferred_element_type=jnp.float32)
    dprob = jnp.einsum("qd,kd->qk", g_own, v_own, preferred_element_type=jnp.float32)
    dscore = (probs * (dprob - delta_row)).astype(jnp.bfloat16)
    grad_q = jnp.dot(dscore, k_own, preferred_element_type=jnp.float32) * score_scale
    grad_k = jnp.einsum("qk,qd->kd", dscore, q_own, preferred_element_type=jnp.float32)
    grad_k = grad_k * score_scale

    back = jnp.stack(
        [g.astype(jnp.bfloat16).reshape(blocks, block_rows, width) for g in (grad_q, grad_k, grad_v)],
        axis=2,
    )
    back = exchange(back.swapaxes(0, 1).reshape(owners, blocks, 3 * width))
    back = back.reshape(owners * blocks, 3 * width)[place]
    back = exchange(back.reshape(owners, blocks, 3 * width))
    back = back.swapaxes(0, 1).reshape(rows_dev, 3 * width)

    member = ((row_cluster % CLUS_DEV)[None, :] == jnp.arange(CLUS_DEV)[:, None]).astype(
        jnp.bfloat16
    )
    partial_sums = jnp.dot(member, k_own, preferred_element_type=jnp.float32)
    whole_sums = lax.psum(partial_sums, "head")
    centroids = whole_sums / jnp.sqrt(
        jnp.mean(whole_sums * whole_sums, axis=1, keepdims=True) + 1e-06
    )
    return (*jnp.split(back, 3, axis=1), centroids)


def solution(mesh):
    placed = (P("ctx", "head"), P("ctx", "head"), P("ctx", "head"), P("ctx", "head"), P("ctx"))
    return jax.shard_map(
        shards,
        mesh=mesh,
        in_specs=placed,
        out_specs=(P("ctx", "head"), P("ctx", "head"), P("ctx", "head"), P("ctx", None)),
        check_vma=False,
    )
```

time: 461 us -> 181 us (0.39)
  waiting for transfers between devices: 344 us -> 62.5 us
  blocking collectives: 10.6 us -> 46.8 us
  local copies, waits for them, and re-layouts: 36.4 us -> 13.5 us
  starting transfers between devices: 58.6 us -> 43.1 us
  other arithmetic: 5.44 us -> 10.7 us
    all_to_all x8 -> x4, waiting for transfers between devices: 344 us -> 62.5 us  [exchange(): lax.all_to_all(pieces, 'ctx', split_axis=0, concat_axis=0, tiled=True)]
    unnamed x0 -> x1, blocking collectives: none -> 36.2 us
    all_to_all x8 -> x4, starting transfers between devices: 58.6 us -> 43.1 us  [exchange(): lax.all_to_all(pieces, 'ctx', split_axis=0, concat_axis=0, tiled=True)]
    scatter x8 -> x0, local copies, waits for them, and re-layouts: 15.1 us -> none  [the longest x4 8.28 us: pack(): return jnp.zeros((slot_count, block_rows, width), source.dtype).at[target...]
    another operation x7 -> x3, local copies, waits for them, and re-layouts: 8.89 us -> 0.27 us  [shards(): jnp.stack([g.astype(jnp.bfloat16).reshape(blocks, block_rows, width) for...]
    sort x1 -> x2, other arithmetic: 2.04 us -> 7.54 us  [the longest x1 3.77 us: shards(): order = jnp.argsort(all_ids // CLUS_DEV, stable=True)]
  transfers between devices with their start and end apart: 8 -> 4, of which waited for: 8 -> 3; matrix products, arithmetic and copies ran while one was open for 7% -> 8% of each run, Pallas kernels for 0% -> 0%
where the time goes in v1:
time: 181 us; the launch traced here: 180 us
  waiting for transfers between devices  62.5 us (35%)
  blocking collectives  46.8 us (26%)
  starting transfers between devices  43.1 us (24%)
  local copies, waits for them, and re-layouts  13.5 us (7%)
  other arithmetic  10.7 us (6%)
  matrix products  2.01 us (1%)
    all_to_all x4, waiting for transfers between devices, exchange(): lax.all_to_all(pieces, 'ctx', split_axis=0, concat_axis=0, tiled=True)  62.5 us
    all_to_all x4, starting transfers between devices, exchange(): lax.all_to_all(pieces, 'ctx', split_axis=0, concat_axis=0, tiled=True)  43.1 us
    unnamed x1, blocking collectives  36.2 us
    psum x1, blocking collectives, shards(): whole_sums = lax.psum(partial_sums, 'head')  10.6 us
    sort x1, other arithmetic, shards(): order = jnp.argsort(all_ids // CLUS_DEV, stable=True)  3.77 us
    sort x1, other arithmetic, shards(): place = jnp.argsort(order, stable=True)  3.77 us
  transfers between devices with their start and end apart: 4, of which 3 were waited for; matrix products, arithmetic and copies ran while one was open for 8% of the time, Pallas kernels for 0%

profile of v1, /device:TPU:6, one launch (start us, length us, event | category | flops | bytes accessed | tf_op | source)
XLA Modules:
  0.0 180.1 jit_solution(10880854704314528611)
XLA Ops:
  0.6 1.2 maximum_bitcast_fusion
  1.8 1.1 copy.32
  2.9 18.7 %all-to-all-start = ((bf16[64,8,512]{2,1,0:T(8,128)(2,1)}), bf16[64,8,512]{2,1,0:T(8,128)(2,1)S(1)}, u32[]{:S(2)}, u32[]{:S(2)}) async-start(bf16[64,8,512]{2,1,0:T(8,128)(2,1)} %bitcast.29), calls=%async_computation | async-start | bytes 1048576 | tf_op jit(solution)/shard_map/all_to_all | solution.py:13
  21.7 1.3 dynamic-slice
  23.6 0.6 copy-done
  24.3 0.2 dynamic-update-slice
  24.4 36.2 %all-reduce = s32[512]{0:T(512)S(1)} all-reduce(s32[512]{0:T(512)S(1)} %dynamic-update-slice), channel_id=1, replica_groups=mesh['ctx'=64,'head'=8] {'ctx'}, use_global_device_ids=true, to_apply=%add | all-reduce | flops 512 | bytes 4096
  60.7 3.8 %sort.31 = (s32[512]{0:T(512)}, s32[512]{0:T(512)S(1)}) sort(s32[512]{0:T(512)S(1)} %add_select_fusion.1, s32[512]{0:T(512)S(1)} %iota.18), dimensions={0}, to_apply=%region_0.1 | sort | flops 4608 | bytes 8192 | tf_op jit(solution)/shard_map/jit(argsort)/sort | solution.py:23
  64.5 2.6 %gather_fusion.1 = bf16[512,512]{1,0:T(8,128)(2,1)} fusion(bf16[512,512]{1,0:T(8,128)(2,1)S(1)} %bitcast.30, s32[1024]{0:T(1024)S(1)} %pad_clamp_fusion.1), kind=kCustom, calls=%fused_computation.1 | custom fusion | bytes 1050624 | tf_op jit(solution)/shard_map/gather | solution.py:31
  67.1 13.3 %all-to-all-start.1 = ((bf16[64,8,512]{2,1,0:T(8,128)(2,1)}), bf16[64,8,512]{2,1,0:T(8,128)(2,1)S(1)}, u32[]{:S(2)}, u32[]{:S(2)}) async-start(bf16[64,8,512]{2,1,0:T(8,128)(2,1)} %bitcast.8), calls=%async_computation.1 | async-start | bytes 1048576 | tf_op jit(solution)/shard_map/all_to_all | solution.py:13
  80.3 3.5 %gather_fusion = s32[512]{0:T(512)S(1)} fusion(s32[512]{0:T(512)S(1)} %all-reduce, s32[1024]{0:T(1024)S(1)} %pad_clamp_fusion.1), kind=kCustom, calls=%fused_computation | custom fusion | bytes 6144 | tf_op jit(solution)/shard_map/gather | solution.py:25
  84.1 26.1 %all-to-all-done.1 = bf16[64,8,512]{2,1,0:T(8,128)(2,1)S(1)} async-done(((bf16[64,8,512]{2,1,0:T(8,128)(2,1)}), bf16[64,8,512]{2,1,0:T(8,128)(2,1)S(1)}, u32[]{:S(2)}, u32[]{:S(2)}) %all-to-all-start.1) | async-done | bytes 524320 | tf_op jit(solution)/shard_map/all_to_all | solution.py:13
  110.2 0.2 copy.22
  110.3 0.3 fusion.25
  110.7 0.2 fusion.8
  110.9 0.2 fusion.9
  111.1 0.3 convolution_convert_fusion
  111.5 0.3 fusion.5
  111.8 0.3 fusion.2
  112.1 0.3 fusion.4
  112.4 0.3 fusion.3
  113.0 0.8 maximum_bitcast_fusion.1
  113.9 5.8 %all-to-all-start.2 = ((bf16[64,8,384]{2,1,0:T(8,128)(2,1)}), bf16[64,8,384]{2,1,0:T(8,128)(2,1)S(1)}, u32[]{:S(2)}, u32[]{:S(2)}) async-start(bf16[64,8,384]{2,1,0:T(8,128)(2,1)} %maximum_bitcast_fusion.1), calls=%async_computation.2 | async-start | bytes 786432 | tf_op jit(solution)/shard_map/all_to_all | solution.py:13
  119.7 3.8 %sort.32 = (s32[512]{0:T(512)}, s32[512]{0:T(512)S(1)}) sort(s32[512]{0:T(512)S(1)} %get-tuple-element.6, s32[512]{0:T(512)S(1)} %iota.19), dimensions={0}, to_apply=%region_4.5 | sort | flops 4608 | bytes 8192 | tf_op jit(solution)/shard_map/jit(argsort)/sort | solution.py:24
  123.5 22.1 %all-to-all-done.2 = bf16[64,8,384]{2,1,0:T(8,128)(2,1)S(1)} async-done(((bf16[64,8,384]{2,1,0:T(8,128)(2,1)}), bf16[64,8,384]{2,1,0:T(8,128)(2,1)S(1)}, u32[]{:S(2)}, u32[]{:S(2)}) %all-to-all-start.2) | async-done | bytes 393248 | tf_op jit(solution)/shard_map/all_to_all | solution.py:13
  145.6 2.6 %gather_fusion.2 = bf16[512,384]{1,0:T(8,128)(2,1)} fusion(bf16[512,384]{1,0:T(8,128)(2,1)S(1)} %bitcast.31, s32[1024]{0:T(1024)S(1)} %pad_clamp_fusion), kind=kCustom, calls=%fused_computation.2 | custom fusion | bytes 788480 | tf_op jit(solution)/shard_map/gather | solution.py:61
  148.2 5.3 %all-to-all-start.3 = ((bf16[64,8,384]{2,1,0:T(8,128)(2,1)}), bf16[64,8,384]{2,1,0:T(8,128)(2,1)S(1)}, u32[]{:S(2)}, u32[]{:S(2)}) async-start(bf16[64,8,384]{2,1,0:T(8,128)(2,1)} %bitcast.18), calls=%async_computation.3 | async-start | bytes 786432 | tf_op jit(solution)/shard_map/all_to_all | solution.py:13
  153.5 0.1 fusion.14
  153.6 10.6 %psum.7 = f32[4,128]{1,0:T(4,128)S(1)} all-reduce(f32[4,128]{1,0:T(4,128)S(1)} %fusion.14), channel_id=1, replica_groups=mesh['ctx'=64,'head'=8] {'head'}, use_global_device_ids=true, to_apply=%region_5.6 | all-reduce | flops 512 | bytes 4096 | tf_op jit(solution)/shard_map/psum | solution.py:69
  164.3 0.7 broadcast_divide_fusion
  165.0 14.3 %all-to-all-done.3 = bf16[64,8,384]{2,1,0:T(8,128)(2,1)S(1)} async-done(((bf16[64,8,384]{2,1,0:T(8,128)(2,1)}), bf16[64,8,384]{2,1,0:T(8,128)(2,1)S(1)}, u32[]{:S(2)}, u32[]{:S(2)}) %all-to-all-start.3) | async-done | bytes 393248 | tf_op jit(solution)/shard_map/all_to_all | solution.py:13
  179.3 0.8 fusion.24
  (22 shorter events, 0.9 us)
Async XLA Ops:
  2.9 61.5 %all-to-all-start = ((bf16[64,8,512]{2,1,0:T(8,128)(2,1)}), bf16[64,8,512]{2,1,0:T(8,128)(2,1)S(1)}, u32[]{:S(2)}, u32[]{:S(2)}) async-start(bf16[64,8,512]{2,1,0:T(8,128)(2,1)} %bitcast.29), calls=%async_computation | async-start | bytes 1048576 | tf_op jit(solution)/shard_map/all_to_all | solution.py:13
  23.6 0.7 copy-start
  67.1 43.1 %all-to-all-start.1 = ((bf16[64,8,512]{2,1,0:T(8,128)(2,1)}), bf16[64,8,512]{2,1,0:T(8,128)(2,1)S(1)}, u32[]{:S(2)}, u32[]{:S(2)}) async-start(bf16[64,8,512]{2,1,0:T(8,128)(2,1)} %bitcast.8), calls=%async_computation.1 | async-start | bytes 1048576 | tf_op jit(solution)/shard_map/all_to_all | solution.py:13
  113.9 31.7 %all-to-all-start.2 = ((bf16[64,8,384]{2,1,0:T(8,128)(2,1)}), bf16[64,8,384]{2,1,0:T(8,128)(2,1)S(1)}, u32[]{:S(2)}, u32[]{:S(2)}) async-start(bf16[64,8,384]{2,1,0:T(8,128)(2,1)} %maximum_bitcast_fusion.1), calls=%async_computation.2 | async-start | bytes 786432 | tf_op jit(solution)/shard_map/all_to_all | solution.py:13
  148.2 31.1 %all-to-all-start.3 = ((bf16[64,8,384]{2,1,0:T(8,128)(2,1)}), bf16[64,8,384]{2,1,0:T(8,128)(2,1)S(1)}, u32[]{:S(2)}, u32[]{:S(2)}) async-start(bf16[64,8,384]{2,1,0:T(8,128)(2,1)} %bitcast.18), calls=%async_computation.3 | async-start | bytes 786432 | tf_op jit(solution)/shard_map/all_to_all | solution.py:13

commit v2 on v1

v2 whole, which is shorter than its diff:
```python
import functools
import math

import jax
import jax.numpy as jnp
from jax import lax
from jax.experimental import pallas as pl
from jax.experimental.pallas import tpu as pltpu
from jax.sharding import PartitionSpec as P

HDIM = 128
CLUS_DEV = 4
BLOCKS = 8
TILE = 16
RING_Y = 4
MESH = pl.DeviceIdType.MESH
NT = (((1,), (1,)), ((), ()))
F32 = jnp.float32
BF16 = jnp.bfloat16

IDS, IN_A, IN_B, OWN_A, OWN_B, GV, GQK, BACK_V, BACK_QK, CEN = range(10)


def iota(shape, dim):
    return lax.broadcasted_iota(jnp.int32, shape, dim)


def onehot(mask):
    return jnp.where(mask, 1.0, 0.0).astype(BF16)


def piece_row(r, block_rows):
    return ((r >> 1) & (BLOCKS - 1)) * block_rows + 2 * (r >> 4) + (r & 1)


def lanes(column, width):
    return jnp.concatenate([column] * (width // HDIM), axis=1) if width > HDIM else column


def kernel(
    n_ctx, n_head,
    q_ref, k_ref, v_ref, g_ref, id_ref,
    dq_ref, dk_ref, dv_ref, cen_ref,
    pack, ids_all, idc, in1, in2, own, res, mid1, mid2, back,
    sort_mat, unsort_mat, probs, dscore, k_t, cen_buf, send_sem, recv_sem,
):
    me = lax.axis_index("ctx")
    head = lax.axis_index("head")
    core = head % 2
    my_z, my_y = me // RING_Y, me % RING_Y
    n_z = n_ctx // RING_Y
    pairs = n_ctx // 2
    rows = BLOCKS * n_ctx
    grows = TILE * n_ctx
    block_rows = n_ctx
    scale = 1.0 / math.sqrt(HDIM)

    def peer(i):
        m = 2 * (i // 8) + i % 2
        dz = n_z // 2 + (1 - 2 * (m % 2)) * ((m + 1) // 2)
        dy = (i // 2 + 1) % RING_Y
        return ((my_z + dz) % n_z) * RING_Y + (my_y + dy) % RING_Y

    def half_tile(p):
        return (p // RING_Y // 2) * RING_Y + p % RING_Y

    def in_half(p):
        return (p // RING_Y) % 2 == core

    def send(src, dst, phase, p):
        pltpu.make_async_remote_copy(
            src_ref=src, dst_ref=dst, send_sem=send_sem.at[phase], recv_sem=recv_sem.at[phase],
            device_id={"ctx": p}, device_id_type=MESH,
        ).start()

    def await_copy(ref, sem):
        pltpu.make_async_copy(ref, ref, sem).wait()

    barrier = pltpu.get_barrier_semaphore()

    @pl.loop(0, n_ctx - 1)
    def _(i):
        pl.semaphore_signal(barrier, 1, device_id={"ctx": peer(i)}, device_id_type=MESH)

    @pl.loop(1, n_head)
    def _(i):
        pl.semaphore_signal(
            barrier, 1, device_id={"head": (head + i) % n_head}, device_id_type=MESH
        )

    chunk = min(128, rows)
    every = jnp.concatenate([q_ref[...], k_ref[...], v_ref[...], g_ref[...]], axis=1)

    @pl.loop(0, rows // chunk)
    def _(c):
        source = piece_row(iota((chunk, rows), 0) + c * chunk, block_rows)
        picked = jnp.dot(
            onehot(source == iota((chunk, rows), 1)), every, preferred_element_type=F32
        ).astype(BF16)
        tiles = chunk // TILE
        for a in range(4):
            pack[pl.ds(a * pairs + c * tiles, tiles)] = picked[
                :, a * HDIM : (a + 1) * HDIM
            ].reshape(tiles, TILE, HDIM)

    ids_all[me] = id_ref[...]
    in1[0, me] = pack[me]
    in1[1, me] = pack[n_ctx + me]

    pl.semaphore_wait(barrier, n_ctx - 1 + n_head - 1)

    @pl.loop(0, n_ctx - 1)
    def _(i):
        p = peer(i)
        send(id_ref, ids_all.at[me], IDS, p)
        send(pack.at[p], in1.at[0, me], IN_A, p)

    @pl.loop(0, n_ctx - 1)
    def _(i):
        p = peer(i)
        send(pack.at[n_ctx + p], in1.at[1, me], IN_B, p)

    await_copy(ids_all.at[pl.ds(0, n_ctx - 1)], recv_sem.at[IDS])
    id_rows = ids_all[...].reshape(n_ctx, HDIM).astype(BF16)
    spread = jnp.dot(
        onehot((iota((grows, n_ctx), 0) >> 4) == iota((grows, n_ctx), 1)),
        id_rows, preferred_element_type=F32,
    )
    keep = ((iota((grows, HDIM), 0) >> 1) & (BLOCKS - 1)) == iota((grows, HDIM), 1)
    spread = jnp.where(keep, spread, 0.0).astype(BF16)
    idc[...] = jnp.dot(spread, jnp.ones((HDIM, HDIM), BF16), preferred_element_type=F32)
    id_lane = lax.dot_general(jnp.ones((8, HDIM), BF16), spread, NT, preferred_element_type=F32)
    owner_lane = jnp.floor(id_lane[0:1] * (1.0 / CLUS_DEV))

    step = min(128, grows)

    def rank(c, before):
        owner = jnp.floor(idc[pl.ds(c * step, step), :] * (1.0 / CLUS_DEV))
        same = lanes(owner, grows) == owner_lane
        row = (iota((step, grows), 0) + c * step) >> 1
        column = iota((step, grows), 1) >> 1
        before = before + jnp.sum(
            jnp.where(same & (row < column), 1.0, 0.0), axis=0, keepdims=True
        )
        ahead = jnp.dot(
            onehot(same & (column < row)), jnp.ones((grows, HDIM), BF16),
            preferred_element_type=F32,
        )
        parity = (iota((step, HDIM), 0) & 1).astype(F32)
        place = TILE * owner + ahead + parity
        unsort_mat[pl.ds(c * step, step), :] = onehot(
            lanes(place, grows) == iota((step, grows), 1).astype(F32)
        )
        return before

    before = lax.fori_loop(0, grows // step, rank, jnp.zeros((1, grows), F32))
    place_lane = TILE * owner_lane + before + (iota((1, grows), 1) & 1).astype(F32)

    @pl.loop(0, grows // step)
    def _(c):
        row = (iota((step, grows), 0) + c * step).astype(F32)
        sort_mat[pl.ds(c * step, step), :] = onehot(row == place_lane)

    id_tile = jnp.dot(
        sort_mat[pl.ds(pl.multiple_of(me * TILE, TILE), TILE), :], idc[...].astype(BF16),
        preferred_element_type=F32,
    )
    id_own = jnp.concatenate([id_tile] * pairs, axis=0)
    id_own_lane = lax.dot_general(
        onehot(iota((8, HDIM), 1) == 0), id_own.astype(BF16), NT, preferred_element_type=F32
    )

    wide = min(256, grows)

    def permute(mat, src, dst, which):
        data = src[which].reshape(grows, HDIM)

        @pl.loop(0, grows // wide)
        def _(c):
            moved = jnp.dot(
                mat[pl.ds(c * wide, wide), :], data, preferred_element_type=F32
            ).astype(BF16)
            dst[which, pl.ds(c * (wide // TILE), wide // TILE)] = moved.reshape(
                wide // TILE, TILE, HDIM
            )

    for which, (arrive, leave) in enumerate(((IN_A, OWN_A), (IN_B, OWN_B))):
        await_copy(in1.at[which, pl.ds(0, n_ctx - 1)], recv_sem.at[arrive])
        permute(sort_mat, in1, in2, which)
        own[which, me] = in2[which, me]

        @pl.loop(0, n_ctx - 1)
        def _(i):
            p = peer(i)
            send(in2.at[which, p], own.at[which, me], leave, p)

    await_copy(own.at[0, pl.ds(0, n_ctx - 1)], recv_sem.at[OWN_A])
    q_own = own[0, pl.ds(0, pairs)].reshape(rows, HDIM)
    k_own = own[0, pl.ds(pairs, pairs)].reshape(rows, HDIM)
    part = min(256, rows)

    for c in range(rows // part):
        cut = slice(c * part, (c + 1) * part)
        scores = (
            lax.dot_general(k_own, q_own[cut], NT, preferred_element_type=F32) * scale
        )
        key_pos = piece_row(iota((rows, part), 0), block_rows)
        query_pos = piece_row(iota((rows, part), 1) + c * part, block_rows)
        allowed = (lanes(id_own, part)[:, :part] == id_own_lane[0:1, cut]) & (key_pos <= query_pos)
        scores = jnp.where(allowed, scores, -jnp.inf)
        exponent = jnp.exp(scores - jnp.max(scores, axis=0, keepdims=True))
        probs[:, cut] = exponent * (1.0 / jnp.sum(exponent, axis=0, keepdims=True))

    local = (id_own_lane - (CLUS_DEV * me).astype(F32)) == iota((8, rows), 0).astype(F32)
    cen_buf[head] = jnp.dot(onehot(local), k_own, preferred_element_type=F32)

    @pl.loop(1, n_head)
    def _(i):
        pltpu.make_async_remote_copy(
            src_ref=cen_buf.at[head], dst_ref=cen_buf.at[head],
            send_sem=send_sem.at[CEN], recv_sem=recv_sem.at[CEN],
            device_id={"head": (head + i) % n_head}, device_id_type=MESH,
        ).start()

    k_t[...] = k_own.astype(F32).T.astype(BF16)

    await_copy(own.at[1, pl.ds(0, n_ctx - 1)], recv_sem.at[OWN_B])
    v_own = own[1, pl.ds(0, pairs)].reshape(rows, HDIM)
    g_own = own[1, pl.ds(pairs, pairs)].reshape(rows, HDIM)

    values_grad = jnp.dot(probs[...].astype(BF16), g_own, preferred_element_type=F32)
    res[pl.ds(2 * pairs, pairs)] = values_grad.astype(BF16).reshape(pairs, TILE, HDIM)

    @pl.when(in_half(me))
    def _():
        mid1[1, me] = res[2 * pairs + half_tile(me)]

    @pl.loop(0, n_ctx - 1)
    def _(i):
        p = peer(i)

        @pl.when(in_half(p))
        def _():
            send(res.at[2 * pairs + half_tile(p)], mid1.at[1, me], GV, p)

    for c in range(rows // part):
        cut = slice(c * part, (c + 1) * part)
        dprob = lax.dot_general(v_own, g_own[cut], NT, preferred_element_type=F32)
        prob = probs[:, cut]
        delta = jnp.sum(prob.astype(BF16).astype(F32) * dprob, axis=0, keepdims=True)
        dscore[:, cut] = (prob * (dprob - delta)).astype(BF16)

    keys_grad = jnp.dot(dscore[...], q_own, preferred_element_type=F32) * scale
    res[pl.ds(pairs, pairs)] = keys_grad.astype(BF16).reshape(pairs, TILE, HDIM)
    queries_grad = jnp.dot(k_t[...], dscore[...], preferred_element_type=F32) * scale
    res[pl.ds(0, pairs)] = queries_grad.T.astype(BF16).reshape(pairs, TILE, HDIM)
    mid1[0, me] = res[me]

    @pl.loop(0, n_ctx - 1)
    def _(i):
        p = peer(i)
        send(res.at[p], mid1.at[0, me], GQK, p)

    @pl.when(in_half(me))
    def _():
        await_copy(mid1.at[1, pl.ds(0, n_ctx - 1)], recv_sem.at[GV])
        permute(unsort_mat, mid1, mid2, 1)
        back[2 * pairs + half_tile(me)] = mid2[1, me]

        @pl.loop(0, n_ctx - 1)
        def _(i):
            p = peer(i)
            send(mid2.at[1, p], back.at[2 * pairs + half_tile(me)], BACK_V, p)

    await_copy(mid1.at[0, pl.ds(0, n_ctx - 1)], recv_sem.at[GQK])
    permute(unsort_mat, mid1, mid2, 0)
    back[me] = mid2[0, me]

    @pl.loop(0, n_ctx - 1)
    def _(i):
        p = peer(i)
        send(mid2.at[0, p], back.at[me], BACK_QK, p)

    await_copy(cen_buf.at[pl.ds(0, n_head - 1)], recv_sem.at[CEN])
    whole = cen_buf[0]
    for h in range(1, n_head):
        whole = whole + cen_buf[h]
    centroids = whole / jnp.sqrt(jnp.mean(whole * whole, axis=1, keepdims=True) + 1e-06)
    cen_ref[...] = centroids[:CLUS_DEV]

    def unpack(first, out):
        data = back[pl.ds(first, pairs)].reshape(rows, HDIM)

        @pl.loop(0, rows // chunk)
        def _(c):
            source = piece_row(iota((chunk, rows), 1), block_rows)
            picked = jnp.dot(
                onehot(source == iota((chunk, rows), 0) + c * chunk), data,
                preferred_element_type=F32,
            )
            out[pl.ds(c * chunk, chunk), :] = picked.astype(BF16)

    @pl.when(in_half(me))
    def _():
        await_copy(back.at[pl.ds(2 * pairs, pairs - 1)], recv_sem.at[BACK_V])
        await_copy(res.at[pl.ds(2 * pairs, pairs - 1)], send_sem.at[GV])
        await_copy(mid2.at[1, pl.ds(0, n_ctx - 1)], send_sem.at[BACK_V])

    @pl.when(jnp.logical_not(in_half(me)))
    def _():
        await_copy(back.at[pl.ds(2 * pairs, pairs)], recv_sem.at[BACK_V])
        await_copy(res.at[pl.ds(2 * pairs, pairs)], send_sem.at[GV])

    unpack(2 * pairs, dv_ref)
    await_copy(back.at[pl.ds(0, n_ctx - 1)], recv_sem.at[BACK_QK])
    unpack(0, dq_ref)
    unpack(pairs, dk_ref)

    await_copy(ids_all.at[pl.ds(0, n_ctx - 1)], send_sem.at[IDS])
    await_copy(pack.at[pl.ds(0, n_ctx - 1)], send_sem.at[IN_A])
    await_copy(pack.at[pl.ds(0, n_ctx - 1)], send_sem.at[IN_B])
    await_copy(in2.at[0, pl.ds(0, n_ctx - 1)], send_sem.at[OWN_A])
    await_copy(in2.at[1, pl.ds(0, n_ctx - 1)], send_sem.at[OWN_B])
    await_copy(res.at[pl.ds(0, n_ctx - 1)], send_sem.at[GQK])
    await_copy(mid2.at[0, pl.ds(0, n_ctx - 1)], send_sem.at[BACK_QK])
    await_copy(cen_buf.at[pl.ds(0, n_head - 1)], send_sem.at[CEN])


def shards(queries, keys, values, out_grad, cluster_ids):
    n_ctx, n_head = lax.axis_size("ctx"), lax.axis_size("head")
    rows = queries.shape[0]
    pairs, grows = n_ctx // 2, TILE * n_ctx
    id_row = jnp.pad(cluster_ids.astype(F32), (0, HDIM - BLOCKS)).reshape(1, HDIM)
    vmem = pl.BlockSpec(memory_space=pltpu.VMEM)
    grad = jax.ShapeDtypeStruct((rows, HDIM), BF16)
    return pl.pallas_call(
        functools.partial(kernel, n_ctx, n_head),
        out_shape=(grad, grad, grad, jax.ShapeDtypeStruct((CLUS_DEV, HDIM), F32)),
        in_specs=[vmem] * 5,
        out_specs=(vmem,) * 4,
        scratch_shapes=[
            pltpu.VMEM((4 * pairs, TILE, HDIM), BF16),
            pltpu.VMEM((n_ctx, 1, HDIM), F32),
            pltpu.VMEM((grows, HDIM), F32),
            pltpu.VMEM((2, n_ctx, TILE, HDIM), BF16),
            pltpu.VMEM((2, n_ctx, TILE, HDIM), BF16),
            pltpu.VMEM((2, n_ctx, TILE, HDIM), BF16),
            pltpu.VMEM((3 * pairs, TILE, HDIM), BF16),
            pltpu.VMEM((2, n_ctx, TILE, HDIM), BF16),
            pltpu.VMEM((2, n_ctx, TILE, HDIM), BF16),
            pltpu.VMEM((3 * pairs, TILE, HDIM), BF16),
            pltpu.VMEM((grows, grows), BF16),
            pltpu.VMEM((grows, grows), BF16),
            pltpu.VMEM((rows, rows), F32),
            pltpu.VMEM((rows, rows), BF16),
            pltpu.VMEM((HDIM, rows), BF16),
            pltpu.VMEM((n_head, 8, HDIM), F32),
            pltpu.SemaphoreType.DMA((10,)),
            pltpu.SemaphoreType.DMA((10,)),
        ],
        compiler_params=pltpu.CompilerParams(
            collective_id=0, has_side_effects=True, vmem_limit_bytes=48 * 2**20
        ),
        name="routing_attention",
    )(queries, keys, values, out_grad, id_row)


def solution(mesh):
    placed = (P("ctx", "head"), P("ctx", "head"), P("ctx", "head"), P("ctx", "head"), P("ctx"))
    return jax.shard_map(
        shards,
        mesh=mesh,
        in_specs=placed,
        out_specs=(P("ctx", "head"), P("ctx", "head"), P("ctx", "head"), P("ctx", None)),
        check_vma=False,
    )
```

time: 181 us -> 114 us (0.63)
  Pallas kernels: 0 us -> 105 us
  waiting for transfers between devices: 62.5 us -> 0 us
  blocking collectives: 46.8 us -> 0 us
  starting transfers between devices: 43.1 us -> 0 us
  other arithmetic: 10.7 us -> 0.66 us
  local copies, waits for them, and re-layouts: 13.5 us -> 6.17 us
  matrix products: 2.01 us -> 0 us
    pallas_call x0 -> x1, Pallas kernels: none -> 105 us  [shards(): pl.pallas_call(functools.partial(kernel, n_ctx, n_head), out_shape=(grad,...]
    all_to_all x4 -> x0, waiting for transfers between devices: 62.5 us -> none  [exchange(): lax.all_to_all(pieces, 'ctx', split_axis=0, concat_axis=0, tiled=True)]
    all_to_all x4 -> x0, starting transfers between devices: 43.1 us -> none  [exchange(): lax.all_to_all(pieces, 'ctx', split_axis=0, concat_axis=0, tiled=True)]
    unnamed x1 -> x0, blocking collectives: 36.2 us -> none
    psum x1 -> x0, blocking collectives: 10.6 us -> none  [shards(): whole_sums = lax.psum(partial_sums, 'head')]
    gather x3 -> x0, local copies, waits for them, and re-layouts: 8.68 us -> none  [the longest x1 3.49 us: shards(): row_ids = lax.dynamic_slice_in_dim(all_ids[order], me * blocks, blocks)]
    sort x2 -> x0, other arithmetic: 7.54 us -> none  [the longest x1 3.77 us: shards(): order = jnp.argsort(all_ids // CLUS_DEV, stable=True)]
    unnamed x7 -> x12, local copies, waits for them, and re-layouts: 2.23 us -> 6.16 us
  transfers between devices with their start and end apart: 4 -> 0, of which waited for: 3 -> 0; matrix products, arithmetic and copies ran while one was open for 8% -> 0% of each run, Pallas kernels for 0% -> 0%
where the time goes in v2:
time: 114 us; the launch traced here: 113 us
  Pallas kernels  105 us (92%)
  local copies, waits for them, and re-layouts  6.17 us (5%)
    pallas_call x1, Pallas kernels, shards(): pl.pallas_call(functools.partial(kernel, n_ctx, n_head), out_shape=(grad,...  105 us
    unnamed x12, local copies, waits for them, and re-layouts  6.16 us

profile of v2, /device:TPU:6, one launch (start us, length us, event | category | flops | bytes accessed | tf_op | source)
XLA Modules:
  0.0 112.7 jit_solution(7635590805656061429)
XLA Ops:
  0.6 0.7 convert_element_type.5
  1.3 0.0 copy-start
  1.3 0.9 copy-done
  2.2 0.0 copy-start.1
  2.2 0.9 copy-done.1
  3.1 0.0 copy-start.2
  3.1 0.9 copy-done.2
  4.0 0.0 copy-start.3
  4.0 0.9 copy-done.3
  4.9 105.2 %routing_attention.1 = (bf16[512,128]{1,0:T(8,128)(2,1)S(1)}, bf16[512,128]{1,0:T(8,128)(2,1)S(1)}, bf16[512,128]{1,0:T(8,128)(2,1)S(1)}, f32[4,128]{1,0:T(4,128)S(1)}) custom-call(bf16[512,128]{1,0:T(8,128)(2,1)S(1)} %copy-done, bf16[512,128]{1,0:T(8,128)(2,1)S(1)} %copy-done.1, bf16[512,128]{1,0:T(8,128)(2,1)S(1)} %copy-done.2, ...), custom_call_target="tpu_custom_call" | custom-call | tf_op jit(solution)/shard_map/routing_attention/pallas_call | solution.py:336
  110.2 0.7 copy.13
  110.8 0.7 copy.14
  111.5 0.7 copy.15
  112.1 0.6 copy.16
  (1 shorter events, 0.0 us)
Async XLA Ops:
  1.3 0.9 copy-start
  2.2 0.9 copy-start.1
  3.1 0.9 copy-start.2
  4.0 0.9 copy-start.3

commit v3 on v2

--- a/solution.py
+++ b/solution.py
@@ -18,7 +18,7 @@
 F32 = jnp.float32
 BF16 = jnp.bfloat16
 
-IDS, IN_A, IN_B, OWN_A, OWN_B, GV, GQK, BACK_V, BACK_QK, CEN = range(10)
+IDS, IN_A, IN_B, OWN_A, OWN_V, OWN_G, GV, GQK, BACK_V, BACK_QK, CEN = range(11)
 
 
 def iota(shape, dim):
@@ -35,14 +35,27 @@
 
 def lanes(column, width):
     return jnp.concatenate([column] * (width // HDIM), axis=1) if width > HDIM else column
+
+
+def unpack(tiles, out):
+    rows = tiles.shape[0] * TILE
+    data = tiles.reshape(rows, HDIM)
+    chunk = min(256, rows)
+    for c in range(rows // chunk):
+        source = piece_row(iota((chunk, rows), 1), rows // BLOCKS)
+        picked = jnp.dot(
+            onehot(source == iota((chunk, rows), 0) + c * chunk), data,
+            preferred_element_type=F32,
+        )
+        out[pl.ds(c * chunk, chunk), :] = picked.astype(BF16)
 
 
 def kernel(
     n_ctx, n_head,
     q_ref, k_ref, v_ref, g_ref, id_ref,
-    dq_ref, dk_ref, dv_ref, cen_ref,
-    pack, ids_all, idc, in1, in2, own, res, mid1, mid2, back,
-    sort_mat, unsort_mat, probs, dscore, k_t, cen_buf, send_sem, recv_sem,
+    back, dv_ref, cen_ref,
+    staged, id_words, id_row, pack, ids_all, idc, in1, in2, own, res, mid1, mid2, back_v,
+    sort_mat, unsort_mat, probs, probs_low, dscore, k_t, cen_buf, load_sem, send_sem, recv_sem,
 ):
     me = lax.axis_index("ctx")
     head = lax.axis_index("head")
@@ -64,8 +77,8 @@
     def half_tile(p):
         return (p // RING_Y // 2) * RING_Y + p % RING_Y
 
-    def in_half(p):
-        return (p // RING_Y) % 2 == core
+    def half(p):
+        return (p // RING_Y + core + 1) % 2
 
     def send(src, dst, phase, p):
         pltpu.make_async_remote_copy(
@@ -88,8 +101,17 @@
             barrier, 1, device_id={"head": (head + i) % n_head}, device_id_type=MESH
         )
 
+    loads = [
+        pltpu.make_async_copy(ref, staged.at[a], load_sem.at[a])
+        for a, ref in enumerate((q_ref, k_ref, v_ref, g_ref))
+    ] + [pltpu.make_async_copy(id_ref, id_words, load_sem.at[4])]
+    for load in loads:
+        load.start()
+    for load in loads:
+        load.wait()
+
     chunk = min(128, rows)
-    every = jnp.concatenate([q_ref[...], k_ref[...], v_ref[...], g_ref[...]], axis=1)
+    every = jnp.concatenate([staged[a] for a in range(4)], axis=1)
 
     @pl.loop(0, rows // chunk)
     def _(c):
@@ -103,22 +125,30 @@
                 :, a * HDIM : (a + 1) * HDIM
             ].reshape(tiles, TILE, HDIM)
 
-    ids_all[me] = id_ref[...]
+    words = jnp.zeros((1, HDIM), jnp.int32)
+    for b in range(BLOCKS):
+        words = jnp.where(iota((1, HDIM), 1) == b, id_words[b], words)
+    id_row[...] = words.astype(F32)
+    ids_all[me] = id_row[...]
+
+    def second(p):
+        return n_ctx + half(p) * pairs + half_tile(p)
+
     in1[0, me] = pack[me]
-    in1[1, me] = pack[n_ctx + me]
+    in1[1, me] = pack[second(me)]
 
     pl.semaphore_wait(barrier, n_ctx - 1 + n_head - 1)
 
     @pl.loop(0, n_ctx - 1)
     def _(i):
         p = peer(i)
-        send(id_ref, ids_all.at[me], IDS, p)
+        send(id_row, ids_all.at[me], IDS, p)
         send(pack.at[p], in1.at[0, me], IN_A, p)
 
     @pl.loop(0, n_ctx - 1)
     def _(i):
         p = peer(i)
-        send(pack.at[n_ctx + p], in1.at[1, me], IN_B, p)
+        send(pack.at[second(p)], in1.at[1, me], IN_B, p)
 
     await_copy(ids_all.at[pl.ds(0, n_ctx - 1)], recv_sem.at[IDS])
     id_rows = ids_all[...].reshape(n_ctx, HDIM).astype(BF16)
@@ -184,15 +214,23 @@
                 wide // TILE, TILE, HDIM
             )
 
-    for which, (arrive, leave) in enumerate(((IN_A, OWN_A), (IN_B, OWN_B))):
-        await_copy(in1.at[which, pl.ds(0, n_ctx - 1)], recv_sem.at[arrive])
-        permute(sort_mat, in1, in2, which)
-        own[which, me] = in2[which, me]
+    def hand_out(which, slot, phase):
+        own[which, slot] = in2[which, me]
 
         @pl.loop(0, n_ctx - 1)
         def _(i):
             p = peer(i)
-            send(in2.at[which, p], own.at[which, me], leave, p)
+            send(in2.at[which, p], own.at[which, slot], phase, p)
+
+    await_copy(in1.at[0, pl.ds(0, n_ctx - 1)], recv_sem.at[IN_A])
+    permute(sort_mat, in1, in2, 0)
+    hand_out(0, me, OWN_A)
+    await_copy(in1.at[1, pl.ds(0, n_ctx - 1)], recv_sem.at[IN_B])
+    permute(sort_mat, in1, in2, 1)
+
+    @pl.when(half(me) == 1)
+    def _():
+        hand_out(1, pairs + half_tile(me), OWN_G)
 
     await_copy(own.at[0, pl.ds(0, n_ctx - 1)], recv_sem.at[OWN_A])
     q_own = own[0, pl.ds(0, pairs)].reshape(rows, HDIM)
@@ -211,6 +249,10 @@
         exponent = jnp.exp(scores - jnp.max(scores, axis=0, keepdims=True))
         probs[:, cut] = exponent * (1.0 / jnp.sum(exponent, axis=0, keepdims=True))
 
+    @pl.when(half(me) == 0)
+    def _():
+        hand_out(1, half_tile(me), OWN_V)
+
     local = (id_own_lane - (CLUS_DEV * me).astype(F32)) == iota((8, rows), 0).astype(F32)
     cen_buf[head] = jnp.dot(onehot(local), k_own, preferred_element_type=F32)
 
@@ -224,14 +266,23 @@
 
     k_t[...] = k_own.astype(F32).T.astype(BF16)
 
-    await_copy(own.at[1, pl.ds(0, n_ctx - 1)], recv_sem.at[OWN_B])
-    v_own = own[1, pl.ds(0, pairs)].reshape(rows, HDIM)
+    def await_half(first, remote, sem):
+        @pl.when(half(me) == remote)
+        def _():
+            await_copy(own.at[1, pl.ds(first, pairs)], sem)
+
+        @pl.when(half(me) == 1 - remote)
+        def _():
+            await_copy(own.at[1, pl.ds(first, pairs - 1)], sem)
+
+    probs_low[...] = probs[...].astype(BF16)
+    await_half(pairs, 0, recv_sem.at[OWN_G])
     g_own = own[1, pl.ds(pairs, pairs)].reshape(rows, HDIM)
 
-    values_grad = jnp.dot(probs[...].astype(BF16), g_own, preferred_element_type=F32)
+    values_grad = jnp.dot(probs_low[...], g_own, preferred_element_type=F32)
     res[pl.ds(2 * pairs, pairs)] = values_grad.astype(BF16).reshape(pairs, TILE, HDIM)
 
-    @pl.when(in_half(me))
+    @pl.when(half(me) == 1)
     def _():
         mid1[1, me] = res[2 * pairs + half_tile(me)]
 
@@ -239,15 +290,18 @@
     def _(i):
         p = peer(i)
 
-        @pl.when(in_half(p))
+        @pl.when(half(p) == 1)
         def _():
             send(res.at[2 * pairs + half_tile(p)], mid1.at[1, me], GV, p)
+
+    await_half(0, 1, recv_sem.at[OWN_V])
+    v_own = own[1, pl.ds(0, pairs)].reshape(rows, HDIM)
 
     for c in range(rows // part):
         cut = slice(c * part, (c + 1) * part)
         dprob = lax.dot_general(v_own, g_own[cut], NT, preferred_element_type=F32)
         prob = probs[:, cut]
-        delta = jnp.sum(prob.astype(BF16).astype(F32) * dprob, axis=0, keepdims=True)
+        delta = jnp.sum(probs_low[:, cut].astype(F32) * dprob, axis=0, keepdims=True)
         dscore[:, cut] = (prob * (dprob - delta)).astype(BF16)
 
     keys_grad = jnp.dot(dscore[...], q_own, preferred_element_type=F32) * scale
@@ -261,16 +315,16 @@
         p = peer(i)
         send(res.at[p], mid1.at[0, me], GQK, p)
 
-    @pl.when(in_half(me))
+    @pl.when(half(me) == 1)
     def _():
         await_copy(mid1.at[1, pl.ds(0, n_ctx - 1)], recv_sem.at[GV])
         permute(unsort_mat, mid1, mid2, 1)
-        back[2 * pairs + half_tile(me)] = mid2[1, me]
+        back_v[half_tile(me)] = mid2[1, me]
 
         @pl.loop(0, n_ctx - 1)
         def _(i):
             p = peer(i)
-            send(mid2.at[1, p], back.at[2 * pairs + half_tile(me)], BACK_V, p)
+            send(mid2.at[1, p], back_v.at[half_tile(me)], BACK_V, p)
 
     await_copy(mid1.at[0, pl.ds(0, n_ctx - 1)], recv_sem.at[GQK])
     permute(unsort_mat, mid1, mid2, 0)
@@ -288,57 +342,63 @@
     centroids = whole / jnp.sqrt(jnp.mean(whole * whole, axis=1, keepdims=True) + 1e-06)
     cen_ref[...] = centroids[:CLUS_DEV]
 
-    def unpack(first, out):
-        data = back[pl.ds(first, pairs)].reshape(rows, HDIM)
-
-        @pl.loop(0, rows // chunk)
-        def _(c):
-            source = piece_row(iota((chunk, rows), 1), block_rows)
-            picked = jnp.dot(
-                onehot(source == iota((chunk, rows), 0) + c * chunk), data,
-                preferred_element_type=F32,
-            )
-            out[pl.ds(c * chunk, chunk), :] = picked.astype(BF16)
-
-    @pl.when(in_half(me))
-    def _():
-        await_copy(back.at[pl.ds(2 * pairs, pairs - 1)], recv_sem.at[BACK_V])
+    @pl.when(half(me) == 1)
+    def _():
+        await_copy(back_v.at[pl.ds(0, pairs - 1)], recv_sem.at[BACK_V])
         await_copy(res.at[pl.ds(2 * pairs, pairs - 1)], send_sem.at[GV])
         await_copy(mid2.at[1, pl.ds(0, n_ctx - 1)], send_sem.at[BACK_V])
 
-    @pl.when(jnp.logical_not(in_half(me)))
-    def _():
-        await_copy(back.at[pl.ds(2 * pairs, pairs)], recv_sem.at[BACK_V])
+    @pl.when(half(me) == 0)
+    def _():
+        await_copy(back_v.at[pl.ds(0, pairs)], recv_sem.at[BACK_V])
         await_copy(res.at[pl.ds(2 * pairs, pairs)], send_sem.at[GV])
 
-    unpack(2 * pairs, dv_ref)
-    await_copy(back.at[pl.ds(0, n_ctx - 1)], recv_sem.at[BACK_QK])
-    unpack(0, dq_ref)
-    unpack(pairs, dk_ref)
-
+    unpack(back_v[...], dv_ref)
     await_copy(ids_all.at[pl.ds(0, n_ctx - 1)], send_sem.at[IDS])
     await_copy(pack.at[pl.ds(0, n_ctx - 1)], send_sem.at[IN_A])
     await_copy(pack.at[pl.ds(0, n_ctx - 1)], send_sem.at[IN_B])
     await_copy(in2.at[0, pl.ds(0, n_ctx - 1)], send_sem.at[OWN_A])
-    await_copy(in2.at[1, pl.ds(0, n_ctx - 1)], send_sem.at[OWN_B])
+    await_copy(in2.at[1, pl.ds(0, n_ctx - 1)], send_sem.at[OWN_V + half(me)])
     await_copy(res.at[pl.ds(0, n_ctx - 1)], send_sem.at[GQK])
     await_copy(mid2.at[0, pl.ds(0, n_ctx - 1)], send_sem.at[BACK_QK])
     await_copy(cen_buf.at[pl.ds(0, n_head - 1)], send_sem.at[CEN])
+    await_copy(back.at[pl.ds(0, n_ctx - 1)], recv_sem.at[BACK_QK])
+
+
+def finish(back, dv_in, cen_in, dq_out, dk_out, dv_out, cen_out, grads, sem):
+    pairs = back.shape[0] // 2
+    stores = [
+        pltpu.make_async_copy(dv_in, dv_out, sem.at[0]),
+        pltpu.make_async_copy(cen_in, cen_out, sem.at[1]),
+        pltpu.make_async_copy(grads.at[0], dq_out, sem.at[2]),
+        pltpu.make_async_copy(grads.at[1], dk_out, sem.at[3]),
+    ]
+    stores[0].start()
+    stores[1].start()
+    for a in range(2):
+        unpack(back[pl.ds(a * pairs, pairs)], grads.at[a])
+        stores[2 + a].start()
+    for store in stores:
+        store.wait()
 
 
 def shards(queries, keys, values, out_grad, cluster_ids):
     n_ctx, n_head = lax.axis_size("ctx"), lax.axis_size("head")
     rows = queries.shape[0]
     pairs, grows = n_ctx // 2, TILE * n_ctx
-    id_row = jnp.pad(cluster_ids.astype(F32), (0, HDIM - BLOCKS)).reshape(1, HDIM)
     vmem = pl.BlockSpec(memory_space=pltpu.VMEM)
+    hbm = pl.BlockSpec(memory_space=pltpu.HBM)
     grad = jax.ShapeDtypeStruct((rows, HDIM), BF16)
-    return pl.pallas_call(
+    centroid = jax.ShapeDtypeStruct((CLUS_DEV, HDIM), F32)
+    back, dv, cen = pl.pallas_call(
         functools.partial(kernel, n_ctx, n_head),
-        out_shape=(grad, grad, grad, jax.ShapeDtypeStruct((CLUS_DEV, HDIM), F32)),
-        in_specs=[vmem] * 5,
-        out_specs=(vmem,) * 4,
+        out_shape=(jax.ShapeDtypeStruct((n_ctx, TILE, HDIM), BF16), grad, centroid),
+        in_specs=[hbm] * 5,
+        out_specs=(vmem,) * 3,
         scratch_shapes=[
+            pltpu.VMEM((4, rows, HDIM), BF16),
+            pltpu.SMEM((BLOCKS,), jnp.int32),
+            pltpu.VMEM((1, HDIM), F32),
             pltpu.VMEM((4 * pairs, TILE, HDIM), BF16),
             pltpu.VMEM((n_ctx, 1, HDIM), F32),
             pltpu.VMEM((grows, HDIM), F32),
@@ -348,21 +408,34 @@
             pltpu.VMEM((3 * pairs, TILE, HDIM), BF16),
             pltpu.VMEM((2, n_ctx, TILE, HDIM), BF16),
             pltpu.VMEM((2, n_ctx, TILE, HDIM), BF16),
-            pltpu.VMEM((3 * pairs, TILE, HDIM), BF16),
+            pltpu.VMEM((pairs, TILE, HDIM), BF16),
             pltpu.VMEM((grows, grows), BF16),
             pltpu.VMEM((grows, grows), BF16),
             pltpu.VMEM((rows, rows), F32),
             pltpu.VMEM((rows, rows), BF16),
+            pltpu.VMEM((rows, rows), BF16),
             pltpu.VMEM((HDIM, rows), BF16),
             pltpu.VMEM((n_head, 8, HDIM), F32),
-            pltpu.SemaphoreType.DMA((10,)),
-            pltpu.SemaphoreType.DMA((10,)),
+            pltpu.SemaphoreType.DMA((5,)),
+            pltpu.SemaphoreType.DMA((11,)),
+            pltpu.SemaphoreType.DMA((11,)),
         ],
         compiler_params=pltpu.CompilerParams(
-            collective_id=0, has_side_effects=True, vmem_limit_bytes=48 * 2**20
+            collective_id=0, has_side_effects=True
         ),
         name="routing_attention",
-    )(queries, keys, values, out_grad, id_row)
+    )(queries, keys, values, out_grad, cluster_ids)
+    return pl.pallas_call(
+        finish,
+        out_shape=(grad, grad, grad, centroid),
+        in_specs=[vmem] * 3,
+        out_specs=(hbm,) * 4,
+        scratch_shapes=[
+            pltpu.VMEM((2, rows, HDIM), BF16),
+            pltpu.SemaphoreType.DMA((4,)),
+        ],
+        name="finish",
+    )(back, dv, cen)
 
 
 def solution(mesh):

time: 114 us -> 106 us (0.930)
  local copies, waits for them, and re-layouts: 6.17 us -> 0 us
    unnamed x12 -> x0, local copies, waits for them, and re-layouts: 6.16 us -> none
    pallas_call x1 -> x2, Pallas kernels: 105 us -> 104 us  [the longest x1 102 us: shards(): pl.pallas_call(functools.partial(kernel, n_ctx, n_head), out_shape=(jax.S...]
where the time goes in v3:
time: 106 us; the launch traced here: 105 us
  Pallas kernels  104 us (98%)
    pallas_call x1, Pallas kernels, shards(): pl.pallas_call(functools.partial(kernel, n_ctx, n_head), out_shape=(jax.S...  102 us
    pallas_call x1, Pallas kernels, shards(): pl.pallas_call(finish, out_shape=(grad, grad, grad, centroid), in_specs=[...  2.17 us

profile of v3, /device:TPU:6, one launch (start us, length us, event | category | flops | bytes accessed | tf_op | source)
XLA Modules:
  0.0 104.9 jit_solution(5853234961887057113)
XLA Ops:
  0.6 102.1 %routing_attention.1 = (bf16[64,16,128]{2,1,0:T(8,128)(2,1)}, bf16[512,128]{1,0:T(8,128)(2,1)}, f32[4,128]{1,0:T(4,128)}) custom-call(bf16[512,128]{1,0:T(8,128)(2,1)} %q_ref.1, bf16[512,128]{1,0:T(8,128)(2,1)} %k_ref.1, bf16[512,128]{1,0:T(8,128)(2,1)} %v_ref.1, bf16[512,128]{1,0:T(8,128)(2,1)} %g_ref.1, s32[8]{0:T(128)} %id_ref.1), custom_call_target="tpu_custom_call" | custom-call | tf_op jit(solution)/shard_map/routing_attention/pallas_call | solution.py:393
  102.7 2.2 %finish.1 = (bf16[512,128]{1,0:T(8,128)(2,1)}, bf16[512,128]{1,0:T(8,128)(2,1)}, bf16[512,128]{1,0:T(8,128)(2,1)}, f32[4,128]{1,0:T(4,128)}) custom-call(bf16[64,16,128]{2,1,0:T(8,128)(2,1)} %get-tuple-element.7.back, bf16[512,128]{1,0:T(8,128)(2,1)} %get-tuple-element.8.dv_in, f32[4,128]{1,0:T(4,128)} %get-tuple-element.9.cen_in), custom_call_target="tpu_custom_call" | custom-call | tf_op jit(solution)/shard_map/finish/pallas_call | solution.py:428

commit v4 on v3

--- a/solution.py
+++ b/solution.py
@@ -18,7 +18,7 @@
 F32 = jnp.float32
 BF16 = jnp.bfloat16
 
-IDS, IN_A, IN_B, OWN_A, OWN_V, OWN_G, GV, GQK, BACK_V, BACK_QK, CEN = range(11)
+IDS, IN_A, IN_B, OWN_A, OWN_V, OWN_G, GV, GQK, BACK_V, BACK_QK, CEN, SHARE = range(12)
 
 
 def iota(shape, dim):
@@ -37,17 +37,18 @@
     return jnp.concatenate([column] * (width // HDIM), axis=1) if width > HDIM else column
 
 
-def unpack(tiles, out):
-    rows = tiles.shape[0] * TILE
-    data = tiles.reshape(rows, HDIM)
+def unpack(tiles, outs):
+    rows = tiles[0].shape[0] * TILE
+    data = jnp.concatenate([t.reshape(rows, HDIM) for t in tiles], axis=1)
     chunk = min(256, rows)
     for c in range(rows // chunk):
         source = piece_row(iota((chunk, rows), 1), rows // BLOCKS)
         picked = jnp.dot(
             onehot(source == iota((chunk, rows), 0) + c * chunk), data,
             preferred_element_type=F32,
-        )
-        out[pl.ds(c * chunk, chunk), :] = picked.astype(BF16)
+        ).astype(BF16)
+        for a, out in enumerate(outs):
+            out[pl.ds(c * chunk, chunk), :] = picked[:, a * HDIM : (a + 1) * HDIM]
 
 
 def kernel(
@@ -55,7 +56,7 @@
     q_ref, k_ref, v_ref, g_ref, id_ref,
     back, dv_ref, cen_ref,
     staged, id_words, id_row, pack, ids_all, idc, in1, in2, own, res, mid1, mid2, back_v,
-    sort_mat, unsort_mat, probs, probs_low, dscore, k_t, cen_buf, load_sem, send_sem, recv_sem,
+    sort_mat, unsort_mat, probs, probs_low, dscore, k_t, cen_buf, cen_own, dv_own, load_sem, send_sem, recv_sem,
 ):
     me = lax.axis_index("ctx")
     head = lax.axis_index("head")
@@ -86,6 +87,12 @@
             device_id={"ctx": p}, device_id_type=MESH,
         ).start()
 
+    def send_head(src, dst, phase, h):
+        pltpu.make_async_remote_copy(
+            src_ref=src, dst_ref=dst, send_sem=send_sem.at[phase], recv_sem=recv_sem.at[phase],
+            device_id={"head": h}, device_id_type=MESH,
+        ).start()
+
     def await_copy(ref, sem):
         pltpu.make_async_copy(ref, ref, sem).wait()
 
@@ -129,7 +136,12 @@
     for b in range(BLOCKS):
         words = jnp.where(iota((1, HDIM), 1) == b, id_words[b], words)
     id_row[...] = words.astype(F32)
-    ids_all[me] = id_row[...]
+    collects = me % n_head == head
+
+    @pl.when(collects)
+    def _():
+        ids_all[me] = id_row[...]
+
 
     def second(p):
         return n_ctx + half(p) * pairs + half_tile(p)
@@ -142,7 +154,14 @@
     @pl.loop(0, n_ctx - 1)
     def _(i):
         p = peer(i)
-        send(id_row, ids_all.at[me], IDS, p)
+
+        @pl.when(p % n_head == head)
+        def _():
+            send(id_row, ids_all.at[me], IDS, p)
+
+    @pl.loop(0, n_ctx - 1)
+    def _(i):
+        p = peer(i)
         send(pack.at[p], in1.at[0, me], IN_A, p)
 
     @pl.loop(0, n_ctx - 1)
@@ -150,7 +169,18 @@
         p = peer(i)
         send(pack.at[second(p)], in1.at[1, me], IN_B, p)
 
-    await_copy(ids_all.at[pl.ds(0, n_ctx - 1)], recv_sem.at[IDS])
+    @pl.when(collects)
+    def _():
+        await_copy(ids_all.at[pl.ds(0, n_ctx - 1)], recv_sem.at[IDS])
+
+        @pl.loop(1, n_head)
+        def _(i):
+            send_head(ids_all, ids_all, SHARE, (head + i) % n_head)
+
+    @pl.when(jnp.logical_not(collects))
+    def _():
+        await_copy(ids_all, recv_sem.at[SHARE])
+
     id_rows = ids_all[...].reshape(n_ctx, HDIM).astype(BF16)
     spread = jnp.dot(
         onehot((iota((grows, n_ctx), 0) >> 4) == iota((grows, n_ctx), 1)),
@@ -258,11 +288,7 @@
 
     @pl.loop(1, n_head)
     def _(i):
-        pltpu.make_async_remote_copy(
-            src_ref=cen_buf.at[head], dst_ref=cen_buf.at[head],
-            send_sem=send_sem.at[CEN], recv_sem=recv_sem.at[CEN],
-            device_id={"head": (head + i) % n_head}, device_id_type=MESH,
-        ).start()
+        send_head(cen_buf.at[head], cen_buf.at[head], CEN, (head + i) % n_head)
 
     k_t[...] = k_own.astype(F32).T.astype(BF16)
 
@@ -340,7 +366,9 @@
     for h in range(1, n_head):
         whole = whole + cen_buf[h]
     centroids = whole / jnp.sqrt(jnp.mean(whole * whole, axis=1, keepdims=True) + 1e-06)
-    cen_ref[...] = centroids[:CLUS_DEV]
+    cen_own[...] = centroids[:CLUS_DEV]
+    store_cen = pltpu.make_async_copy(cen_own, cen_ref, load_sem.at[1])
+    store_cen.start()
 
     @pl.when(half(me) == 1)
     def _():
@@ -353,8 +381,23 @@
         await_copy(back_v.at[pl.ds(0, pairs)], recv_sem.at[BACK_V])
         await_copy(res.at[pl.ds(2 * pairs, pairs)], send_sem.at[GV])
 
-    unpack(back_v[...], dv_ref)
-    await_copy(ids_all.at[pl.ds(0, n_ctx - 1)], send_sem.at[IDS])
+    unpack([back_v[...]], [dv_own])
+    store_dv = pltpu.make_async_copy(dv_own, dv_ref, load_sem.at[2])
+    store_dv.start()
+    groups = n_ctx // n_head
+
+    @pl.when(collects)
+    def _():
+        await_copy(ids_all.at[pl.ds(0, groups - 1)], send_sem.at[IDS])
+
+        @pl.loop(1, n_head)
+        def _(i):
+            await_copy(ids_all, send_sem.at[SHARE])
+
+    @pl.when(jnp.logical_not(collects))
+    def _():
+        await_copy(ids_all.at[pl.ds(0, groups)], send_sem.at[IDS])
+
     await_copy(pack.at[pl.ds(0, n_ctx - 1)], send_sem.at[IN_A])
     await_copy(pack.at[pl.ds(0, n_ctx - 1)], send_sem.at[IN_B])
     await_copy(in2.at[0, pl.ds(0, n_ctx - 1)], send_sem.at[OWN_A])
@@ -362,24 +405,36 @@
     await_copy(res.at[pl.ds(0, n_ctx - 1)], send_sem.at[GQK])
     await_copy(mid2.at[0, pl.ds(0, n_ctx - 1)], send_sem.at[BACK_QK])
     await_copy(cen_buf.at[pl.ds(0, n_head - 1)], send_sem.at[CEN])
+    store_cen.wait()
+    store_dv.wait()
     await_copy(back.at[pl.ds(0, n_ctx - 1)], recv_sem.at[BACK_QK])
 
 
-def finish(back, dv_in, cen_in, dq_out, dk_out, dv_out, cen_out, grads, sem):
+def finish(back, dv_in, cen_in, dq_out, dk_out, dv_out, cen_out, tiles, grads, cen, load, store):
     pairs = back.shape[0] // 2
+    loads = [
+        pltpu.make_async_copy(back.at[pl.ds(0, pairs)], tiles.at[0], load.at[0]),
+        pltpu.make_async_copy(back.at[pl.ds(pairs, pairs)], tiles.at[1], load.at[1]),
+        pltpu.make_async_copy(dv_in, grads.at[2], load.at[2]),
+        pltpu.make_async_copy(cen_in, cen, load.at[3]),
+    ]
     stores = [
-        pltpu.make_async_copy(dv_in, dv_out, sem.at[0]),
-        pltpu.make_async_copy(cen_in, cen_out, sem.at[1]),
-        pltpu.make_async_copy(grads.at[0], dq_out, sem.at[2]),
-        pltpu.make_async_copy(grads.at[1], dk_out, sem.at[3]),
+        pltpu.make_async_copy(grads.at[0], dq_out, store.at[0]),
+        pltpu.make_async_copy(grads.at[1], dk_out, store.at[1]),
+        pltpu.make_async_copy(grads.at[2], dv_out, store.at[2]),
+        pltpu.make_async_copy(cen, cen_out, store.at[3]),
     ]
-    stores[0].start()
-    stores[1].start()
-    for a in range(2):
-        unpack(back[pl.ds(a * pairs, pairs)], grads.at[a])
-        stores[2 + a].start()
-    for store in stores:
-        store.wait()
+    for copy in loads:
+        copy.start()
+    loads[0].wait()
+    loads[1].wait()
+    unpack([tiles[0], tiles[1]], [grads.at[0], grads.at[1]])
+    for a in range(4):
+        if a > 1:
+            loads[a].wait()
+        stores[a].start()
+    for copy in stores:
+        copy.wait()
 
 
 def shards(queries, keys, values, out_grad, cluster_ids):
@@ -394,7 +449,7 @@
         functools.partial(kernel, n_ctx, n_head),
         out_shape=(jax.ShapeDtypeStruct((n_ctx, TILE, HDIM), BF16), grad, centroid),
         in_specs=[hbm] * 5,
-        out_specs=(vmem,) * 3,
+        out_specs=(vmem, hbm, hbm),
         scratch_shapes=[
             pltpu.VMEM((4, rows, HDIM), BF16),
             pltpu.SMEM((BLOCKS,), jnp.int32),
@@ -416,9 +471,11 @@
             pltpu.VMEM((rows, rows), BF16),
             pltpu.VMEM((HDIM, rows), BF16),
             pltpu.VMEM((n_head, 8, HDIM), F32),
+            pltpu.VMEM((CLUS_DEV, HDIM), F32),
+            pltpu.VMEM((rows, HDIM), BF16),
             pltpu.SemaphoreType.DMA((5,)),
-            pltpu.SemaphoreType.DMA((11,)),
-            pltpu.SemaphoreType.DMA((11,)),
+            pltpu.SemaphoreType.DMA((12,)),
+            pltpu.SemaphoreType.DMA((12,)),
         ],
         compiler_params=pltpu.CompilerParams(
             collective_id=0, has_side_effects=True
@@ -428,10 +485,13 @@
     return pl.pallas_call(
         finish,
         out_shape=(grad, grad, grad, centroid),
-        in_specs=[vmem] * 3,
+        in_specs=[hbm] * 3,
         out_specs=(hbm,) * 4,
         scratch_shapes=[
-            pltpu.VMEM((2, rows, HDIM), BF16),
+            pltpu.VMEM((2, pairs, TILE, HDIM), BF16),
+            pltpu.VMEM((3, rows, HDIM), BF16),
+            pltpu.VMEM((CLUS_DEV, HDIM), F32),
+            pltpu.SemaphoreType.DMA((4,)),
             pltpu.SemaphoreType.DMA((4,)),
         ],
         name="finish",

time: 106 us -> 104 us (0.981)
    pallas_call x1, Pallas kernels: 102 us -> 101 us  [shards(): pl.pallas_call(functools.partial(kernel, n_ctx, n_head), out_shape=(jax.S...]
where the time goes in v4:
time: 104 us; the launch traced here: 103 us
  Pallas kernels  103 us (99%)
    pallas_call x1, Pallas kernels, shards(): pl.pallas_call(functools.partial(kernel, n_ctx, n_head), out_shape=(jax.S...  101 us
    pallas_call x1, Pallas kernels, shards(): pl.pallas_call(finish, out_shape=(grad, grad, grad, centroid), in_specs=[...  2.09 us

profile of v4, /device:TPU:6, one launch (start us, length us, event | category | flops | bytes accessed | tf_op | source)
XLA Modules:
  0.0 103.4 jit_solution(6661576716140356453)
XLA Ops:
  0.6 100.7 %routing_attention.1 = (bf16[64,16,128]{2,1,0:T(8,128)(2,1)}, bf16[512,128]{1,0:T(8,128)(2,1)}, f32[4,128]{1,0:T(4,128)}) custom-call(bf16[512,128]{1,0:T(8,128)(2,1)} %q_ref.1, bf16[512,128]{1,0:T(8,128)(2,1)} %k_ref.1, bf16[512,128]{1,0:T(8,128)(2,1)} %v_ref.1, bf16[512,128]{1,0:T(8,128)(2,1)} %g_ref.1, s32[8]{0:T(128)} %id_ref.1), custom_call_target="tpu_custom_call" | custom-call | tf_op jit(solution)/shard_map/routing_attention/pallas_call | solution.py:448
  101.3 2.1 %finish.1 = (bf16[512,128]{1,0:T(8,128)(2,1)}, bf16[512,128]{1,0:T(8,128)(2,1)}, bf16[512,128]{1,0:T(8,128)(2,1)}, f32[4,128]{1,0:T(4,128)}) custom-call(bf16[64,16,128]{2,1,0:T(8,128)(2,1)} %get-tuple-element.7.back, bf16[512,128]{1,0:T(8,128)(2,1)} %get-tuple-element.8.dv_in, f32[4,128]{1,0:T(4,128)} %get-tuple-element.9.cen_in), custom_call_target="tpu_custom_call" | custom-call | tf_op jit(solution)/shard_map/finish/pallas_call | solution.py:485

commit v5 on v4

--- a/solution.py
+++ b/solution.py
@@ -70,16 +70,16 @@
     scale = 1.0 / math.sqrt(HDIM)
 
     def peer(i):
-        m = 2 * (i // 8) + i % 2
-        dz = n_z // 2 + (1 - 2 * (m % 2)) * ((m + 1) // 2)
-        dy = (i // 2 + 1) % RING_Y
-        return ((my_z + dz) % n_z) * RING_Y + (my_y + dy) % RING_Y
+        odd, step = lax.rem(i, 2), lax.div(i, 8)
+        dz = n_z // 2 + step - odd * (2 * step + 1)
+        dy = lax.div(i, 2) + 1
+        return lax.rem(my_z + dz, n_z) * RING_Y + lax.rem(my_y + dy, RING_Y)
 
     def half_tile(p):
-        return (p // RING_Y // 2) * RING_Y + p % RING_Y
+        return lax.div(p, 2 * RING_Y) * RING_Y + lax.rem(p, RING_Y)
 
     def half(p):
-        return (p // RING_Y + core + 1) % 2
+        return lax.rem(lax.div(p, RING_Y) + core + 1, 2)
 
     def send(src, dst, phase, p):
         pltpu.make_async_remote_copy(
@@ -151,11 +151,11 @@
 
     pl.semaphore_wait(barrier, n_ctx - 1 + n_head - 1)
 
-    @pl.loop(0, n_ctx - 1)
-    def _(i):
-        p = peer(i)
-
-        @pl.when(p % n_head == head)
+    @pl.loop(0, n_ctx // n_head)
+    def _(i):
+        p = i * n_head + head
+
+        @pl.when(p != me)
         def _():
             send(id_row, ids_all.at[me], IDS, p)
 

time: 104 us -> 104 us (level)
  no operation moved by 1% of the time
where the time goes in v5:
time: 104 us; the launch traced here: 103 us
  Pallas kernels  102 us (98%)
    pallas_call x1, Pallas kernels, shards(): pl.pallas_call(functools.partial(kernel, n_ctx, n_head), out_shape=(jax.S...  100 us
    pallas_call x1, Pallas kernels, shards(): pl.pallas_call(finish, out_shape=(grad, grad, grad, centroid), in_specs=[...  2.09 us

profile of v5, /device:TPU:6, one launch (start us, length us, event | category | flops | bytes accessed | tf_op | source)
XLA Modules:
  0.0 103.0 jit_solution(14472906058023251099)
XLA Ops:
  0.6 100.2 %routing_attention.1 = (bf16[64,16,128]{2,1,0:T(8,128)(2,1)}, bf16[512,128]{1,0:T(8,128)(2,1)}, f32[4,128]{1,0:T(4,128)}) custom-call(bf16[512,128]{1,0:T(8,128)(2,1)} %q_ref.1, bf16[512,128]{1,0:T(8,128)(2,1)} %k_ref.1, bf16[512,128]{1,0:T(8,128)(2,1)} %v_ref.1, bf16[512,128]{1,0:T(8,128)(2,1)} %g_ref.1, s32[8]{0:T(128)} %id_ref.1), custom_call_target="tpu_custom_call" | custom-call | tf_op jit(solution)/shard_map/routing_attention/pallas_call | solution.py:448
  100.9 2.1 %finish.1 = (bf16[512,128]{1,0:T(8,128)(2,1)}, bf16[512,128]{1,0:T(8,128)(2,1)}, bf16[512,128]{1,0:T(8,128)(2,1)}, f32[4,128]{1,0:T(4,128)}) custom-call(bf16[64,16,128]{2,1,0:T(8,128)(2,1)} %get-tuple-element.7.back, bf16[512,128]{1,0:T(8,128)(2,1)} %get-tuple-element.8.dv_in, f32[4,128]{1,0:T(4,128)} %get-tuple-element.9.cen_in), custom_call_target="tpu_custom_call" | custom-call | tf_op jit(solution)/shard_map/finish/pallas_call | solution.py:485

commit v6 on v5

--- a/solution.py
+++ b/solution.py
@@ -114,24 +114,27 @@
     ] + [pltpu.make_async_copy(id_ref, id_words, load_sem.at[4])]
     for load in loads:
         load.start()
-    for load in loads:
-        load.wait()
+    for a in (0, 1, 4):
+        loads[a].wait()
 
     chunk = min(128, rows)
-    every = jnp.concatenate([staged[a] for a in range(4)], axis=1)
-
-    @pl.loop(0, rows // chunk)
-    def _(c):
-        source = piece_row(iota((chunk, rows), 0) + c * chunk, block_rows)
-        picked = jnp.dot(
-            onehot(source == iota((chunk, rows), 1)), every, preferred_element_type=F32
-        ).astype(BF16)
-        tiles = chunk // TILE
-        for a in range(4):
-            pack[pl.ds(a * pairs + c * tiles, tiles)] = picked[
-                :, a * HDIM : (a + 1) * HDIM
-            ].reshape(tiles, TILE, HDIM)
-
+
+    def pack_two(first):
+        every = jnp.concatenate([staged[first], staged[first + 1]], axis=1)
+
+        @pl.loop(0, rows // chunk)
+        def _(c):
+            source = piece_row(iota((chunk, rows), 0) + c * chunk, block_rows)
+            picked = jnp.dot(
+                onehot(source == iota((chunk, rows), 1)), every, preferred_element_type=F32
+            ).astype(BF16)
+            tiles = chunk // TILE
+            for a in range(2):
+                pack[pl.ds((first + a) * pairs + c * tiles, tiles)] = picked[
+                    :, a * HDIM : (a + 1) * HDIM
+                ].reshape(tiles, TILE, HDIM)
+
+    pack_two(0)
     words = jnp.zeros((1, HDIM), jnp.int32)
     for b in range(BLOCKS):
         words = jnp.where(iota((1, HDIM), 1) == b, id_words[b], words)
@@ -147,7 +150,6 @@
         return n_ctx + half(p) * pairs + half_tile(p)
 
     in1[0, me] = pack[me]
-    in1[1, me] = pack[second(me)]
 
     pl.semaphore_wait(barrier, n_ctx - 1 + n_head - 1)
 
@@ -163,6 +165,11 @@
     def _(i):
         p = peer(i)
         send(pack.at[p], in1.at[0, me], IN_A, p)
+
+    loads[2].wait()
+    loads[3].wait()
+    pack_two(2)
+    in1[1, me] = pack[second(me)]
 
     @pl.loop(0, n_ctx - 1)
     def _(i):

time: 104 us -> 104 us (level)
  no operation moved by 1% of the time
where the time goes in v6:
time: 104 us; the launch traced here: 103 us
  Pallas kernels  102 us (98%)
    pallas_call x1, Pallas kernels, shards(): pl.pallas_call(functools.partial(kernel, n_ctx, n_head), out_shape=(jax.S...  100 us
    pallas_call x1, Pallas kernels, shards(): pl.pallas_call(finish, out_shape=(grad, grad, grad, centroid), in_specs=[...  2.08 us

profile of v6, /device:TPU:6, one launch (start us, length us, event | category | flops | bytes accessed | tf_op | source)
XLA Modules:
  0.0 103.0 jit_solution(5014920185822587412)
XLA Ops:
  0.6 100.3 %routing_attention.1 = (bf16[64,16,128]{2,1,0:T(8,128)(2,1)}, bf16[512,128]{1,0:T(8,128)(2,1)}, f32[4,128]{1,0:T(4,128)}) custom-call(bf16[512,128]{1,0:T(8,128)(2,1)} %q_ref.1, bf16[512,128]{1,0:T(8,128)(2,1)} %k_ref.1, bf16[512,128]{1,0:T(8,128)(2,1)} %v_ref.1, bf16[512,128]{1,0:T(8,128)(2,1)} %g_ref.1, s32[8]{0:T(128)} %id_ref.1), custom_call_target="tpu_custom_call" | custom-call | tf_op jit(solution)/shard_map/routing_attention/pallas_call | solution.py:455
  100.9 2.1 %finish.1 = (bf16[512,128]{1,0:T(8,128)(2,1)}, bf16[512,128]{1,0:T(8,128)(2,1)}, bf16[512,128]{1,0:T(8,128)(2,1)}, f32[4,128]{1,0:T(4,128)}) custom-call(bf16[64,16,128]{2,1,0:T(8,128)(2,1)} %get-tuple-element.7.back, bf16[512,128]{1,0:T(8,128)(2,1)} %get-tuple-element.8.dv_in, f32[4,128]{1,0:T(4,128)} %get-tuple-element.9.cen_in), custom_call_target="tpu_custom_call" | custom-call | tf_op jit(solution)/shard_map/finish/pallas_call | solution.py:492

commit v7 on v6

--- a/solution.py
+++ b/solution.py
@@ -209,6 +209,57 @@
         before = before + jnp.sum(
             jnp.where(same & (row < column), 1.0, 0.0), axis=0, keepdims=True
         )
+        return before
+
+    before = lax.fori_loop(0, grows // step, rank, jnp.zeros((1, grows), F32))
+    place_lane = TILE * owner_lane + before + (iota((1, grows), 1) & 1).astype(F32)
+
+    @pl.loop(0, grows // step)
+    def _(c):
+        row = (iota((step, grows), 0) + c * step).astype(F32)
+        sort_mat[pl.ds(c * step, step), :] = onehot(row == place_lane)
+
+    id_tile = jnp.dot(
+        sort_mat[pl.ds(pl.multiple_of(me * TILE, TILE), TILE), :], idc[...].astype(BF16),
+        preferred_element_type=F32,
+    )
+    id_own = jnp.concatenate([id_tile] * pairs, axis=0)
+    id_own_lane = lax.dot_general(
+        onehot(iota((8, HDIM), 1) == 0), id_own.astype(BF16), NT, preferred_element_type=F32
+    )
+
+    wide = min(256, grows)
+
+    def permute(mat, src, dst, which):
+        data = src[which].reshape(grows, HDIM)
+
+        @pl.loop(0, grows // wide)
+        def _(c):
+            moved = jnp.dot(
+                mat[pl.ds(c * wide, wide), :], data, preferred_element_type=F32
+            ).astype(BF16)
+            dst[which, pl.ds(c * (wide // TILE), wide // TILE)] = moved.reshape(
+                wide // TILE, TILE, HDIM
+            )
+
+    def hand_out(which, slot, phase):
+        own[which, slot] = in2[which, me]
+
+        @pl.loop(0, n_ctx - 1)
+        def _(i):
+            p = peer(i)
+            send(in2.at[which, p], own.at[which, slot], phase, p)
+
+    await_copy(in1.at[0, pl.ds(0, n_ctx - 1)], recv_sem.at[IN_A])
+    permute(sort_mat, in1, in2, 0)
+    hand_out(0, me, OWN_A)
+
+    @pl.loop(0, grows // step)
+    def _(c):
+        owner = jnp.floor(idc[pl.ds(c * step, step), :] * (1.0 / CLUS_DEV))
+        same = lanes(owner, grows) == owner_lane
+        row = (iota((step, grows), 0) + c * step) >> 1
+        column = iota((step, grows), 1) >> 1
         ahead = jnp.dot(
             onehot(same & (column < row)), jnp.ones((grows, HDIM), BF16),
             preferred_element_type=F32,
@@ -218,50 +269,7 @@
         unsort_mat[pl.ds(c * step, step), :] = onehot(
             lanes(place, grows) == iota((step, grows), 1).astype(F32)
         )
-        return before
-
-    before = lax.fori_loop(0, grows // step, rank, jnp.zeros((1, grows), F32))
-    place_lane = TILE * owner_lane + before + (iota((1, grows), 1) & 1).astype(F32)
-
-    @pl.loop(0, grows // step)
-    def _(c):
-        row = (iota((step, grows), 0) + c * step).astype(F32)
-        sort_mat[pl.ds(c * step, step), :] = onehot(row == place_lane)
-
-    id_tile = jnp.dot(
-        sort_mat[pl.ds(pl.multiple_of(me * TILE, TILE), TILE), :], idc[...].astype(BF16),
-        preferred_element_type=F32,
-    )
-    id_own = jnp.concatenate([id_tile] * pairs, axis=0)
-    id_own_lane = lax.dot_general(
-        onehot(iota((8, HDIM), 1) == 0), id_own.astype(BF16), NT, preferred_element_type=F32
-    )
-
-    wide = min(256, grows)
-
-    def permute(mat, src, dst, which):
-        data = src[which].reshape(grows, HDIM)
-
-        @pl.loop(0, grows // wide)
-        def _(c):
-            moved = jnp.dot(
-                mat[pl.ds(c * wide, wide), :], data, preferred_element_type=F32
-            ).astype(BF16)
-            dst[which, pl.ds(c * (wide // TILE), wide // TILE)] = moved.reshape(
-                wide // TILE, TILE, HDIM
-            )
-
-    def hand_out(which, slot, phase):
-        own[which, slot] = in2[which, me]
-
-        @pl.loop(0, n_ctx - 1)
-        def _(i):
-            p = peer(i)
-            send(in2.at[which, p], own.at[which, slot], phase, p)
-
-    await_copy(in1.at[0, pl.ds(0, n_ctx - 1)], recv_sem.at[IN_A])
-    permute(sort_mat, in1, in2, 0)
-    hand_out(0, me, OWN_A)
+
     await_copy(in1.at[1, pl.ds(0, n_ctx - 1)], recv_sem.at[IN_B])
     permute(sort_mat, in1, in2, 1)
 

time: 104 us -> 103 us (level)
  no operation moved by 1% of the time
where the time goes in v7:
time: 103 us
  Pallas kernels  102 us (99%)
    pallas_call x1, Pallas kernels, shards(): pl.pallas_call(functools.partial(kernel, n_ctx, n_head), out_shape=(jax.S...  99.9 us
    pallas_call x1, Pallas kernels, shards(): pl.pallas_call(finish, out_shape=(grad, grad, grad, centroid), in_specs=[...  2.09 us

profile of v7, /device:TPU:6, one launch (start us, length us, event | category | flops | bytes accessed | tf_op | source)
XLA Modules:
  0.0 102.6 jit_solution(4626853695887086405)
XLA Ops:
  0.6 99.9 %routing_attention.1 = (bf16[64,16,128]{2,1,0:T(8,128)(2,1)}, bf16[512,128]{1,0:T(8,128)(2,1)}, f32[4,128]{1,0:T(4,128)}) custom-call(bf16[512,128]{1,0:T(8,128)(2,1)} %q_ref.1, bf16[512,128]{1,0:T(8,128)(2,1)} %k_ref.1, bf16[512,128]{1,0:T(8,128)(2,1)} %v_ref.1, bf16[512,128]{1,0:T(8,128)(2,1)} %g_ref.1, s32[8]{0:T(128)} %id_ref.1), custom_call_target="tpu_custom_call" | custom-call | tf_op jit(solution)/shard_map/routing_attention/pallas_call | solution.py:463
  100.5 2.1 %finish.1 = (bf16[512,128]{1,0:T(8,128)(2,1)}, bf16[512,128]{1,0:T(8,128)(2,1)}, bf16[512,128]{1,0:T(8,128)(2,1)}, f32[4,128]{1,0:T(4,128)}) custom-call(bf16[64,16,128]{2,1,0:T(8,128)(2,1)} %get-tuple-element.7.back, bf16[512,128]{1,0:T(8,128)(2,1)} %get-tuple-element.8.dv_in, f32[4,128]{1,0:T(4,128)} %get-tuple-element.9.cen_in), custom_call_target="tpu_custom_call" | custom-call | tf_op jit(solution)/shard_map/finish/pallas_call | solution.py:500
